TPU v7x, 32 devices: a whole 2x2x4 slice. The times are simulated.
32 devices in a mesh: tm: 4 (over y, x), games: 4 (over z), member: 2 (over core).
Axes of the slice: x: 2, y: 2, z: 4, core: 2. Of those that a mesh axis runs over, the one named last changes fastest.
Arguments:
- rewards: float32 [32, 16384], P('games', 'tm'), as said below
- dones: int32 [32, 16384], P('games', 'tm'), may hold values 0 or 1
- values: float32 [2, 32, 16384], P('member', 'games', 'tm'), may hold values from -6 to 6
- discount: float32 [32], P('games'), as said below
- trace: float32 [32], P('games'), as said below
Outputs:
- returns: float32 [32, 16384], P('games', 'tm')
- advantages: float32 [32, 16384], P('games', 'tm')
- value_loss: float32 [2, 32], P('member', 'games')
Inputs may be any that keep to these rules, and one draw needn't show every extreme that they name: rewards lie between -3.6 and 3.6. Each discount lies between 1 - 1/30 and 1 - 1/1048576. Each trace lies between 1 - 1/30 and 1 - 1/1048576.
All inputs are finite; a program needn't handle non-finite values. No bound on the sum of `dones` on one device may be relied on, other than what follows from the above.
Results may differ from a plain program's by a relative error of at most 0.0003.
Values sent between devices are 32-bit elements; how exact they have to be, the bound alone decides.
No kernel may reach another device: no remote copies, remote signals or barrier semaphores. Data moves between devices by JAX's collectives and lax.ppermute only.
A program may use at most 64 MiB of HBM per device.

v0:
```python
import functools

import jax
import jax.numpy as jnp
from jax import lax
from jax.experimental import pallas as pl
from jax.experimental.pallas import tpu as pltpu
from jax.sharding import PartitionSpec as P

LANES = 128
SLOT = 16
GROUPS = LANES // SLOT
VMEM = pl.BlockSpec(memory_space=pltpu.VMEM)


def iotas(rows):
    shape = (rows, LANES)
    return (
        lax.broadcasted_iota(jnp.int32, shape, 0),
        lax.broadcasted_iota(jnp.int32, shape, 1),
    )


def spread(column, rows):
    return jnp.broadcast_to(column, (rows, LANES))


def to_column(row, rows):
    sub, lane = iotas(rows)
    padded = jnp.broadcast_to(jnp.pad(row, ((0, 0), (0, LANES - rows))), (rows, LANES))
    return spread(jnp.sum(jnp.where(lane == sub, padded, 0.0), axis=1, keepdims=True), rows)


def local_kernel(
    members, rewards, dones, own, other, discount, trace, scan_out, alpha_out, mean_out, stats_out
):
    rows, moves = rewards.shape
    tiles = moves // LANES
    sub, lane = iotas(rows)
    last_block = lax.axis_index("tm") == lax.axis_size("tm") - 1
    offset_lane = lax.rem(lax.axis_index("games"), GROUPS) * SLOT

    disc = to_column(discount[...], rows)
    lam = to_column(trace[...], rows)
    rate = disc * lam
    boot = disc * (1.0 - lam)

    def tile(ref, j):
        return ref[:, j * LANES : (j + 1) * LANES]

    own_last = own[:, moves - 1 : moves]
    mean_last = (own_last + other[:, moves - 1 : moves]) / members
    reward_last = rewards[:, moves - 1 : moves]
    guess = jnp.where(last_block, 0.0, spread(mean_last - reward_last, rows) / rate)
    own_guess = jnp.where(last_block, 0.0, spread(own_last - reward_last, rows) / rate)
    gap = own_guess - guess

    carry, scale = guess, jnp.ones((rows, LANES), jnp.float32)
    ahead = jnp.zeros((rows, LANES), jnp.float32)
    zero = jnp.zeros((rows, LANES), jnp.float32)
    suu, sua, saa, sqq, sqa = zero, zero, zero, zero, zero
    for j in reversed(range(tiles)):
        mine = tile(own, j)
        mean = (mine + tile(other, j)) / members
        mean_out[:, j * LANES : (j + 1) * LANES] = mean
        shifted = pltpu.roll(mean, LANES - 1, 1)
        following = jnp.where(lane == LANES - 1, ahead, shifted)
        ahead = shifted
        keep = 1.0 - tile(dones, j).astype(jnp.float32)
        a = rate * keep
        b = tile(rewards, j) + boot * keep * following
        step = 1
        while step < LANES:
            inside = lane < LANES - step
            b = b + jnp.where(inside, a, 0.0) * pltpu.roll(b, LANES - step, 1)
            a = jnp.where(inside, a * pltpu.roll(a, LANES - step, 1), a)
            step *= 2
        result = b + a * carry
        alpha = a * scale
        scan_out[:, j * LANES : (j + 1) * LANES] = result
        alpha_out[:, j * LANES : (j + 1) * LANES] = alpha
        a_head, b_head = spread(a[:, :1], rows), spread(b[:, :1], rows)
        carry = b_head + a_head * carry
        scale = a_head * scale
        u = result - mean
        q = mine - result - alpha * gap
        suu += u * u
        sua += u * alpha
        saa += alpha * alpha
        sqq += q * q
        sqa += q * alpha

    def total(x):
        return spread(jnp.sum(x, axis=1, keepdims=True), rows)

    mean_head = spread(mean_out[:, :1], rows)
    entries = (
        carry + (1.0 - lam) / lam * mean_head,
        scale,
        guess,
        total(suu),
        total(sua),
        total(saa),
        own_guess,
        total(sqq),
        total(sqa),
    )
    stats = zero
    for k, entry in enumerate(entries):
        stats = jnp.where(lane == offset_lane + k, entry, stats)
    stats_out[...] = jnp.broadcast_to(stats[None], stats_out.shape)


def final_kernel(
    blocks, groups, moves_all, cells_all, scan, alpha, mean, stats, returns_out, adv_out, loss_out
):
    rows, moves = scan.shape
    tiles = moves // LANES
    sub, lane = iotas(rows)
    block = lax.axis_index("tm")
    group = lax.axis_index("games")
    slot = lax.rem(group, GROUPS) * SLOT

    squares = jnp.zeros((rows, LANES), jnp.float32)
    own_eps = jnp.zeros((rows, LANES), jnp.float32)
    own_loss = jnp.zeros((rows, LANES), jnp.float32)
    for first in range(0, groups, GROUPS):
        last = min(first + GROUPS, groups)
        here = (lane == slot) & (group >= first) & (group < last)
        valid = (lax.rem(lane, SLOT) == 0) & (lane < (last - first) * SLOT)
        ahead = jnp.zeros((rows, LANES), jnp.float32)
        for t in reversed(range(blocks)):
            merged = stats[t * groups + first]
            for g in range(first + 1, last):
                merged = merged + stats[t * groups + g]
            pick = [merged] + [pltpu.roll(merged, LANES - k, 1) for k in range(1, 9)]
            head, slope, guess, suu, sua, saa, own_guess, sqq, sqa = pick
            eps = ahead - guess
            own = ahead - own_guess
            ahead = head + slope * eps
            squares += jnp.where(valid, suu + eps * (2.0 * sua + eps * saa), 0.0)
            own_loss += jnp.where(here, sqq + own * (own * saa - 2.0 * sqa), 0.0)
            own_eps += jnp.where(here & (block == t), eps, 0.0)

    eps = spread(jnp.sum(own_eps, axis=1, keepdims=True), rows)
    total = jnp.sum(jnp.sum(squares, axis=1, keepdims=True), axis=0, keepdims=True)
    norm_scale = jnp.broadcast_to(lax.rsqrt(total / cells_all + 1e-06), (rows, LANES))
    loss = spread(jnp.sum(own_loss, axis=1, keepdims=True), rows)
    loss_row = jnp.sum(jnp.where(lane == sub, loss, 0.0), axis=0, keepdims=True)
    loss_out[...] = loss_row[:, :rows] / moves_all
    for j in range(tiles):
        at = slice(j * LANES, (j + 1) * LANES)
        result = scan[:, at] + alpha[:, at] * eps
        returns_out[:, at] = result
        adv_out[:, at] = (result - mean[:, at]) * norm_scale


def per_device(rewards, dones, values, discount, trace):
    members = lax.axis_size("member")
    blocks = lax.axis_size("tm")
    groups = lax.axis_size("games")
    own = values[0]
    rows, moves = own.shape
    other = None
    for turn in range(1, members):
        got = lax.ppermute(own, "member", [(m, (m + turn) % members) for m in range(members)])
        other = got if other is None else other + got

    block = jax.ShapeDtypeStruct((rows, moves), jnp.float32)
    scan, alpha, mean, stats = pl.pallas_call(
        functools.partial(local_kernel, members),
        out_shape=(
            block,
            block,
            block,
            jax.ShapeDtypeStruct((blocks * groups, rows, LANES), jnp.float32),
        ),
        in_specs=[VMEM] * 6,
        out_specs=(VMEM,) * 4,
        name="local_scan",
    )(rewards, dones, own, other, discount[None], trace[None])
    stats = lax.all_to_all(stats, ("tm", "games"), 0, 0, tiled=True)
    moves_all = moves * blocks
    returns, advantages, loss = pl.pallas_call(
        functools.partial(
            final_kernel, blocks, groups, float(moves_all), float(moves_all * rows * groups)
        ),
        out_shape=(block, block, jax.ShapeDtypeStruct((1, rows), jnp.float32)),
        in_specs=[VMEM] * 4,
        out_specs=(VMEM,) * 3,
        name="finish",
    )(scan, alpha, mean, stats)
    return returns, advantages, loss


def solution(mesh):
    return jax.shard_map(
        per_device,
        mesh=mesh,
        in_specs=(
            P("games", "tm"),
            P("games", "tm"),
            P("member", "games", "tm"),
            P("games"),
            P("games"),
        ),
        out_specs=(P("games", "tm"), P("games", "tm"), P("member", "games")),
        check_vma=False,
    )
```

profile of v0, /device:TPU:0, one launch (start us, length us, event | category | flops | bytes accessed | tf_op | source)
XLA Modules:
  0.0 23.4 jit_solution(10721727739771083907)
XLA Ops:
  0.6 0.6 %collective-permute-start = (f32[8,4096]{1,0:T(8,128)}, f32[8,4096]{1,0:T(8,128)S(1)}, u32[]{:S(2)}, u32[]{:S(2)}) collective-permute-start(f32[8,4096]{1,0:T(8,128)} %bitcast.3), channel_id=1, source_target_pairs={{0,1},{1,0},{2,3},{3,2},{4,5},{5,4},{6,7},{7,6},{8,9},{9,8},{10,11... | collective-permute-start | bytes 393224 | tf_op jit(solution)/shard_map/ppermute | solution.py:166
  1.2 1.2 %collective-permute-done.other = f32[8,4096]{1,0:T(8,128)S(1)} collective-permute-done((f32[8,4096]{1,0:T(8,128)}, f32[8,4096]{1,0:T(8,128)S(1)}, u32[]{:S(2)}, u32[]{:S(2)}) %collective-permute-start) | collective-permute-done | bytes 131104 | tf_op jit(solution)/shard_map/ppermute | solution.py:166
  2.4 0.0 copy-start
  2.4 0.7 %copy-done = f32[8,4096]{1,0:T(8,128)} copy-done((f32[8,4096]{1,0:T(8,128)}, f32[8,4096]{1,0:T(8,128)S(1)}, u32[]{:S(2)}) %copy-start) | copy-done | bytes 131096
  3.0 2.7 %local_scan.1 = (f32[8,4096]{1,0:T(8,128)}, f32[8,4096]{1,0:T(8,128)}, f32[8,4096]{1,0:T(8,128)}, f32[16,8,128]{2,1,0:T(8,128)}) custom-call(f32[8,4096]{1,0:T(8,128)} %rewards.1, s32[8,4096]{1,0:T(8,128)} %dones.1, f32[8,4096]{1,0:T(8,128)} %bitcast.4, f32[8,4096]{1,0:T(8,128)} %copy-done, f32[1,8]{1,0:T(1,128)} %bitcast.5, f32[1,8]{1,0:T(1,128)} %bitcast.6), custom_call_target="tpu_custom_call" | custom-call | tf_op jit(solution)/shard_map/local_scan/pallas_call | solution.py:170
  5.7 15.8 %all_to_all.5.stats = f32[16,8,128]{2,1,0:T(8,128)} all-to-all(f32[16,8,128]{2,1,0:T(8,128)} %get-tuple-element.10), channel_id=1, replica_groups=mesh['tm'=4,'games'=4,'member'=2] {'tm','games'}, dimensions={0} | all-to-all | bytes 131072 | tf_op jit(solution)/shard_map/all_to_all | solution.py:182
  21.5 1.9 %finish.1 = (f32[8,4096]{1,0:T(8,128)}, f32[8,4096]{1,0:T(8,128)}, f32[1,8]{1,0:T(1,128)}) custom-call(f32[8,4096]{1,0:T(8,128)} %get-tuple-element.7.scan, f32[8,4096]{1,0:T(8,128)} %get-tuple-element.8.alpha, f32[8,4096]{1,0:T(8,128)} %get-tuple-element.9.mean, f32[16,8,128]{2,1,0:T(8,128)} %all_to_all.5.stats), custom_call_target="tpu_custom_call" | custom-call | tf_op jit(solution)/shard_map/finish/pallas_call | solution.py:184
Async XLA Ops:
  0.6 1.8 %collective-permute-start = (f32[8,4096]{1,0:T(8,128)}, f32[8,4096]{1,0:T(8,128)S(1)}, u32[]{:S(2)}, u32[]{:S(2)}) collective-permute-start(f32[8,4096]{1,0:T(8,128)} %bitcast.3), channel_id=1, source_target_pairs={{0,1},{1,0},{2,3},{3,2},{4,5},{5,4},{6,7},{7,6},{8,9},{9,8},{10,11... | collective-permute-start | bytes 393224 | tf_op jit(solution)/shard_map/ppermute | solution.py:166
  2.4 0.7 %copy-start = (f32[8,4096]{1,0:T(8,128)}, f32[8,4096]{1,0:T(8,128)S(1)}, u32[]{:S(2)}) copy-start(f32[8,4096]{1,0:T(8,128)S(1)} %collective-permute-done.other) | copy-start | bytes 393220
where the time goes:
time: 23.7 us; the launch traced here: 23.4 us
  blocking collectives  15.8 us (67%)
  Pallas kernels  4.63 us (20%)
  waiting for transfers between devices  1.2 us (5%)
  local copies, waits for them, and re-layouts  0.65 us (3%)
  between operations  0.63 us (3%)
  starting transfers between devices  0.56 us (2%)
    all_to_all x1, blocking collectives, per_device(): stats = lax.all_to_all(stats, ('tm', 'games'), 0, 0, tiled=True)  15.8 us
    pallas_call x1, Pallas kernels, per_device(): pl.pallas_call(functools.partial(local_kernel, members), out_shape=(block...  2.69 us
    pallas_call x1, Pallas kernels, per_device(): pl.pallas_call(functools.partial(final_kernel, blocks, groups, float(move...  1.94 us
    ppermute x1, waiting for transfers between devices, per_device(): lax.ppermute(own, 'member', [(m, (m + turn) % members) for m in range(mem...  1.2 us
    unnamed x2, local copies, waits for them, and re-layouts  0.65 us
    ppermute x1, starting transfers between devices, per_device(): lax.ppermute(own, 'member', [(m, (m + turn) % members) for m in range(mem...  0.56 us
  transfers between devices with their start and end apart: 1, of which 1 were waited for; matrix products, arithmetic and copies ran while one was open for 0% of the time, Pallas kernels for 0%

commit v1 on v0

v1 whole, which is shorter than its diff:
```python
import functools

import jax
import jax.numpy as jnp
from jax import lax
from jax.experimental import pallas as pl
from jax.experimental.pallas import tpu as pltpu
from jax.sharding import PartitionSpec as P

LANES = 128
STEPS = tuple(1 << k for k in range(7))
SLOT = 16
GROUPS = LANES // SLOT
VMEM = pl.BlockSpec(memory_space=pltpu.VMEM)
HBM = pl.BlockSpec(memory_space=pltpu.HBM)
VMEM_LIMIT = 4 << 20


def iotas(rows):
    shape = (rows, LANES)
    return (
        lax.broadcasted_iota(jnp.int32, shape, 0),
        lax.broadcasted_iota(jnp.int32, shape, 1),
    )


def spread(column, rows):
    return jnp.broadcast_to(column, (rows, LANES))


def to_column(row, rows):
    sub, lane = iotas(rows)
    padded = jnp.broadcast_to(jnp.pad(row, ((0, 0), (0, LANES - rows))), (rows, LANES))
    return spread(jnp.sum(jnp.where(lane == sub, padded, 0.0), axis=1, keepdims=True), rows)


def at(j):
    return slice(j * LANES, (j + 1) * LANES)


def decay_kernel(
    rewards, dones, own, discount, trace,
    rewards_out, own_out, gates_out, decay_out, alpha_out, boot_out, heads_out, consts_out,
    dones_in, discount_in, trace_in, sems,
):
    rows, moves = dones_in.shape
    tiles = moves // LANES
    sub, lane = iotas(rows)
    pairs = (
        (discount, discount_in),
        (trace, trace_in),
        (dones, dones_in),
        (own, own_out),
        (rewards, rewards_out),
    )
    copies = [pltpu.make_async_copy(*pair, sems.at[k]) for k, pair in enumerate(pairs)]
    for copy in copies:
        copy.start()
    copies[0].wait()
    copies[1].wait()
    disc = to_column(discount_in[...], rows)
    lam = to_column(trace_in[...], rows)
    rate = disc * lam
    boot = disc * (1.0 - lam)
    consts_out[0] = rate
    consts_out[1] = (1.0 - lam) / lam
    copies[2].wait()
    scale = jnp.ones((rows, LANES), jnp.float32)
    saa = jnp.zeros((rows, LANES), jnp.float32)
    for j in reversed(range(tiles)):
        keep = 1.0 - dones_in[:, at(j)].astype(jnp.float32)
        boot_out[:, at(j)] = boot * keep
        a = rate * keep
        for k, step in enumerate(STEPS):
            inside = lane < LANES - step
            gates_out[k, :, at(j)] = jnp.where(inside, a, 0.0)
            a = jnp.where(inside, a * pltpu.roll(a, LANES - step, 1), a)
        head = spread(a[:, :1], rows)
        alpha = a * scale
        decay_out[:, at(j)] = a
        alpha_out[:, at(j)] = alpha
        heads_out[j] = head
        scale = head * scale
        saa += alpha * alpha
    consts_out[2] = scale
    consts_out[3] = spread(jnp.sum(saa, axis=1, keepdims=True), rows)
    copies[3].wait()
    copies[4].wait()


def local_kernel(
    members, rewards, own, other, gates, decay, alpha, boot, heads, consts,
    scan_out, mean_out, stats_out,
):
    rows, moves = rewards.shape
    tiles = moves // LANES
    sub, lane = iotas(rows)
    last_block = lax.axis_index("tm") == lax.axis_size("tm") - 1
    offset_lane = lax.rem(lax.axis_index("games"), GROUPS) * SLOT

    rate, ratio, slope, saa = consts[0], consts[1], consts[2], consts[3]
    own_last = own[:, moves - 1 : moves]
    mean_last = (own_last + other[:, moves - 1 : moves]) / members
    reward_last = rewards[:, moves - 1 : moves]
    guess = jnp.where(last_block, 0.0, spread(mean_last - reward_last, rows) / rate)
    own_guess = jnp.where(last_block, 0.0, spread(own_last - reward_last, rows) / rate)
    gap = own_guess - guess

    zero = jnp.zeros((rows, LANES), jnp.float32)
    carry, ahead = guess, zero
    suu, sua, sqq, sqa = zero, zero, zero, zero
    for j in reversed(range(tiles)):
        mine = own[:, at(j)]
        mean = (mine + other[:, at(j)]) / members
        mean_out[:, at(j)] = mean
        shifted = pltpu.roll(mean, LANES - 1, 1)
        following = jnp.where(lane == LANES - 1, ahead, shifted)
        ahead = shifted
        b = rewards[:, at(j)] + boot[:, at(j)] * following
        for k, step in enumerate(STEPS):
            b = b + gates[k, :, at(j)] * pltpu.roll(b, LANES - step, 1)
        result = b + decay[:, at(j)] * carry
        scan_out[:, at(j)] = result
        carry = spread(b[:, :1], rows) + heads[j] * carry
        weight = alpha[:, at(j)]
        u = result - mean
        q = mine - result - weight * gap
        suu += u * u
        sua += u * weight
        sqq += q * q
        sqa += q * weight

    def total(x):
        return spread(jnp.sum(x, axis=1, keepdims=True), rows)

    entries = (
        carry + ratio * spread(mean_out[:, :1], rows),
        slope,
        guess,
        total(suu),
        total(sua),
        saa,
        own_guess,
        total(sqq),
        total(sqa),
    )
    stats = zero
    for k, entry in enumerate(entries):
        stats = jnp.where(lane == offset_lane + k, entry, stats)
    stats_out[...] = jnp.broadcast_to(stats[None], stats_out.shape)


def final_kernel(
    blocks, groups, moves_all, cells_all, scan, alpha, mean, stats,
    returns_out, adv_out, loss_out, returns, adv, loss, sems,
):
    rows, moves = scan.shape
    tiles = moves // LANES
    sub, lane = iotas(rows)
    block = lax.axis_index("tm")
    group = lax.axis_index("games")
    slot = lax.rem(group, GROUPS) * SLOT

    squares = jnp.zeros((rows, LANES), jnp.float32)
    own_eps = jnp.zeros((rows, LANES), jnp.float32)
    own_loss = jnp.zeros((rows, LANES), jnp.float32)
    for first in range(0, groups, GROUPS):
        last = min(first + GROUPS, groups)
        here = (lane == slot) & (group >= first) & (group < last)
        valid = (lax.rem(lane, SLOT) == 0) & (lane < (last - first) * SLOT)
        ahead = jnp.zeros((rows, LANES), jnp.float32)
        for t in reversed(range(blocks)):
            merged = stats[t * groups + first]
            for g in range(first + 1, last):
                merged = merged + stats[t * groups + g]
            pick = [merged] + [pltpu.roll(merged, LANES - k, 1) for k in range(1, 9)]
            head, slope, guess, suu, sua, saa, own_guess, sqq, sqa = pick
            eps = ahead - guess
            own = ahead - own_guess
            ahead = head + slope * eps
            squares += jnp.where(valid, suu + eps * (2.0 * sua + eps * saa), 0.0)
            own_loss += jnp.where(here, sqq + own * (own * saa - 2.0 * sqa), 0.0)
            own_eps += jnp.where(here & (block == t), eps, 0.0)

    eps = spread(jnp.sum(own_eps, axis=1, keepdims=True), rows)
    total = jnp.sum(jnp.sum(squares, axis=1, keepdims=True), axis=0, keepdims=True)
    norm_scale = jnp.broadcast_to(lax.rsqrt(total / cells_all + 1e-06), (rows, LANES))
    column = spread(jnp.sum(own_loss, axis=1, keepdims=True), rows)
    loss_row = jnp.sum(jnp.where(lane == sub, column, 0.0), axis=0, keepdims=True)
    loss[...] = loss_row[:, :rows] / moves_all
    copies = [pltpu.make_async_copy(loss, loss_out, sems.at[0])]
    copies[0].start()
    parts = 2
    size = tiles // parts
    for part in range(parts):
        for j in range(part * size, (part + 1) * size):
            result = scan[:, at(j)] + alpha[:, at(j)] * eps
            returns[:, at(j)] = result
            adv[:, at(j)] = (result - mean[:, at(j)]) * norm_scale
        span = pl.ds(part * size * LANES, size * LANES)
        for k, (src, dst) in enumerate(((returns, returns_out), (adv, adv_out))):
            copy = pltpu.make_async_copy(
                src.at[:, span], dst.at[:, span], sems.at[1 + 2 * part + k]
            )
            copy.start()
            copies.append(copy)
    for copy in copies:
        copy.wait()


def per_device(rewards, dones, values, discount, trace):
    members = lax.axis_size("member")
    blocks = lax.axis_size("tm")
    groups = lax.axis_size("games")
    own = values[0]
    rows, moves = own.shape
    tiles = moves // LANES
    other = None
    for turn in range(1, members):
        got = lax.ppermute(own, "member", [(m, (m + turn) % members) for m in range(members)])
        other = got if other is None else other + got

    def array(*shape):
        return jax.ShapeDtypeStruct(shape, jnp.float32)

    params = pltpu.CompilerParams(vmem_limit_bytes=VMEM_LIMIT)
    block = array(rows, moves)
    kept_rewards, kept_own, gates, decay, alpha, boot, heads, consts = pl.pallas_call(
        decay_kernel,
        out_shape=(
            block, block, array(len(STEPS), rows, moves), block, block, block,
            array(tiles, rows, LANES), array(4, rows, LANES),
        ),
        in_specs=[HBM] * 5,
        out_specs=(VMEM,) * 8,
        scratch_shapes=[
            pltpu.VMEM((rows, moves), jnp.int32),
            pltpu.VMEM((1, rows), jnp.float32),
            pltpu.VMEM((1, rows), jnp.float32),
            pltpu.SemaphoreType.DMA((5,)),
        ],
        compiler_params=params,
        cost_estimate=pl.CostEstimate(flops=4000000, bytes_accessed=2000000, transcendentals=0),
        name="decay_scan",
    )(
        *(
            pltpu.with_memory_space_constraint(x, pltpu.HBM)
            for x in (rewards, dones, own, discount[None], trace[None])
        )
    )
    scan, mean, stats = pl.pallas_call(
        functools.partial(local_kernel, members),
        out_shape=(block, block, array(blocks * groups, rows, LANES)),
        in_specs=[VMEM] * 9,
        out_specs=(VMEM,) * 3,
        compiler_params=params,
        name="local_scan",
    )(kept_rewards, kept_own, other, gates, decay, alpha, boot, heads, consts)
    stats = lax.all_to_all(stats, ("tm", "games"), 0, 0, tiled=True)
    moves_all = moves * blocks
    returns, advantages, loss = pl.pallas_call(
        functools.partial(
            final_kernel, blocks, groups, float(moves_all), float(moves_all * rows * groups)
        ),
        out_shape=(block, block, array(1, rows)),
        in_specs=[VMEM] * 4,
        out_specs=(HBM,) * 3,
        scratch_shapes=[
            pltpu.VMEM((rows, moves), jnp.float32),
            pltpu.VMEM((rows, moves), jnp.float32),
            pltpu.VMEM((1, rows), jnp.float32),
            pltpu.SemaphoreType.DMA((5,)),
        ],
        compiler_params=params,
        name="finish",
    )(scan, alpha, mean, stats)
    return returns, advantages, loss


def solution(mesh):
    return jax.shard_map(
        per_device,
        mesh=mesh,
        in_specs=(
            P("games", "tm"),
            P("games", "tm"),
            P("member", "games", "tm"),
            P("games"),
            P("games"),
        ),
        out_specs=(P("games", "tm"), P("games", "tm"), P("member", "games")),
        check_vma=False,
    )
```

time: 23.7 us -> 19.9 us (0.84)
  Pallas kernels: 4.63 us -> 3.4 us
  waiting for transfers between devices: 1.2 us -> 0.01 us
  blocking collectives: 15.8 us -> 15.1 us
  local copies, waits for them, and re-layouts: 0.65 us -> 0 us
    pallas_call x1, Pallas kernels: 2.69 us -> 0.82 us  [per_device(): pl.pallas_call(functools.partial(local_kernel, members), out_shape=(block...]
    pallas_call x0 -> x1, Pallas kernels: none -> 1.65 us  [per_device(): pl.pallas_call(decay_kernel, out_shape=(block, block, array(len(STEPS), r...]
    ppermute x1, waiting for transfers between devices: 1.2 us -> 0.01 us  [per_device(): lax.ppermute(own, 'member', [(m, (m + turn) % members) for m in range(mem...]
    pallas_call x1, Pallas kernels: 1.94 us -> 0.93 us  [per_device(): pl.pallas_call(functools.partial(final_kernel, blocks, groups, float(move...]
    unnamed x2 -> x0, local copies, waits for them, and re-layouts: 0.65 us -> none
    all_to_all x1, blocking collectives: 15.8 us -> 15.1 us  [per_device(): stats = lax.all_to_all(stats, ('tm', 'games'), 0, 0, tiled=True)]
  transfers between devices with their start and end apart: 1 -> 1, of which waited for: 1 -> 0; matrix products, arithmetic and copies ran while one was open for 0% -> 0% of each run, Pallas kernels for 0% -> 8%
where the time goes in v1:
time: 19.9 us; the launch traced here: 19.7 us
  blocking collectives  15.1 us (76%)
  Pallas kernels  3.4 us (17%)
  between operations  0.65 us (3%)
  starting transfers between devices  0.56 us (3%)
    all_to_all x1, blocking collectives, per_device(): stats = lax.all_to_all(stats, ('tm', 'games'), 0, 0, tiled=True)  15.1 us
    pallas_call x1, Pallas kernels, per_device(): pl.pallas_call(decay_kernel, out_shape=(block, block, array(len(STEPS), r...  1.65 us
    pallas_call x1, Pallas kernels, per_device(): pl.pallas_call(functools.partial(final_kernel, blocks, groups, float(move...  0.93 us
    pallas_call x1, Pallas kernels, per_device(): pl.pallas_call(functools.partial(local_kernel, members), out_shape=(block...  0.82 us
    ppermute x1, starting transfers between devices, per_device(): lax.ppermute(own, 'member', [(m, (m + turn) % members) for m in range(mem...  0.56 us
  transfers between devices with their start and end apart: 1, of which 0 were waited for; matrix products, arithmetic and copies ran while one was open for 0% of the time, Pallas kernels for 8%

profile of v1, /device:TPU:0, one launch (start us, length us, event | category | flops | bytes accessed | tf_op | source)
XLA Modules:
  0.0 19.7 jit_solution(5230761093541791173)
XLA Ops:
  0.6 0.6 %collective-permute-start = (f32[8,4096]{1,0:T(8,128)}, f32[8,4096]{1,0:T(8,128)S(1)}, u32[]{:S(2)}, u32[]{:S(2)}) collective-permute-start(f32[8,4096]{1,0:T(8,128)} %bitcast.3), channel_id=1, source_target_pairs={{0,1},{1,0},{2,3},{3,2},{4,5},{5,4},{6,7},{7,6},{8,9},{9,8},{10,11... | collective-permute-start | bytes 393224 | tf_op jit(solution)/shard_map/ppermute | solution.py:220
  1.2 1.7 %decay_scan.1 = (f32[8,4096]{1,0:T(8,128)S(1)}, f32[8,4096]{1,0:T(8,128)S(1)}, f32[7,8,4096]{2,1,0:T(8,128)S(1)}, f32[8,4096]{1,0:T(8,128)S(1)}, f32[8,4096]{1,0...) custom-call(f32[8,4096]{1,0:T(8,128)} %rewards.1, s32[8,4096]{1,0:T(8,128)} %dones.1, ...), custom_call_target="tpu_custom_call" | custom-call | flops 4000000 | bytes 2000000 | tf_op jit(solution)/shard_map/decay_scan/pallas_call | solution.py:228
  2.8 0.0 collective-permute-done.other
  2.9 0.8 %local_scan.1 = (f32[8,4096]{1,0:T(8,128)S(1)}, f32[8,4096]{1,0:T(8,128)S(1)}, f32[16,8,128]{2,1,0:T(8,128)S(1)}) custom-call(f32[8,4096]{1,0:T(8,128)S(1)} %get-tuple-element.14.rewards, f32[8,4096]{1,0:T(8,128)S(1)} %get-tuple-element.15.own, f32[8,4096]{1,0:T(8,128)S(1)} %collective-permute-done.other, f32[7,8,4096]{2,1,0:T(8,128)S(1)} %get-tuple-element.16.gates, ...), custom_call_target="tpu_custom_call" | custom-call | tf_op jit(solution)/shard_map/local_scan/pallas_call | solution.py:251
  3.7 15.1 %all_to_all.5.stats = f32[16,8,128]{2,1,0:T(8,128)S(1)} all-to-all(f32[16,8,128]{2,1,0:T(8,128)S(1)} %get-tuple-element.24), channel_id=1, replica_groups=mesh['tm'=4,'games'=4,'member'=2] {'tm','games'}, dimensions={0} | all-to-all | bytes 131072 | tf_op jit(solution)/shard_map/all_to_all | solution.py:259
  18.8 0.9 %finish.1 = (f32[8,4096]{1,0:T(8,128)}, f32[8,4096]{1,0:T(8,128)}, f32[1,8]{1,0:T(1,128)}) custom-call(f32[8,4096]{1,0:T(8,128)S(1)} %get-tuple-element.22.scan, f32[8,4096]{1,0:T(8,128)S(1)} %get-tuple-element.18.alpha, f32[8,4096]{1,0:T(8,128)S(1)} %get-tuple-element.23.mean, f32[16,8,128]{2,1,0:T(8,128)S(1)} %all_to_all.5.stats), custom_call_target="tpu_custom_call" | custom-call | tf_op jit(solution)/shard_map/finish/pallas_call | solution.py:261
Async XLA Ops:
  0.6 2.2 %collective-permute-start = (f32[8,4096]{1,0:T(8,128)}, f32[8,4096]{1,0:T(8,128)S(1)}, u32[]{:S(2)}, u32[]{:S(2)}) collective-permute-start(f32[8,4096]{1,0:T(8,128)} %bitcast.3), channel_id=1, source_target_pairs={{0,1},{1,0},{2,3},{3,2},{4,5},{5,4},{6,7},{7,6},{8,9},{9,8},{10,11... | collective-permute-start | bytes 393224 | tf_op jit(solution)/shard_map/ppermute | solution.py:220

commit v2 on v1

v2 whole, which is shorter than its diff:
```python
import functools

import jax
import jax.numpy as jnp
from jax import lax
from jax.experimental import pallas as pl
from jax.experimental.pallas import tpu as pltpu
from jax.sharding import PartitionSpec as P

LANES = 128
STEPS = tuple(1 << k for k in range(7))
SLOT = 16
LOSSES = 6
VMEM = pl.BlockSpec(memory_space=pltpu.VMEM)
HBM = pl.BlockSpec(memory_space=pltpu.HBM)
VMEM_LIMIT = 4 << 20


def iotas(rows):
    shape = (rows, LANES)
    return (
        lax.broadcasted_iota(jnp.int32, shape, 0),
        lax.broadcasted_iota(jnp.int32, shape, 1),
    )


def spread(column, rows):
    return jnp.broadcast_to(column, (rows, LANES))


def to_column(row, rows):
    sub, lane = iotas(rows)
    padded = jnp.broadcast_to(jnp.pad(row, ((0, 0), (0, LANES - rows))), (rows, LANES))
    return spread(jnp.sum(jnp.where(lane == sub, padded, 0.0), axis=1, keepdims=True), rows)


def at(j):
    return slice(j * LANES, (j + 1) * LANES)


def decay_kernel(
    rewards, dones, own, discount, trace,
    rewards_out, own_out, gates_out, decay_out, alpha_out, boot_out, heads_out, consts_out,
    dones_in, discount_in, trace_in, sems,
):
    rows, moves = dones_in.shape
    tiles = moves // LANES
    sub, lane = iotas(rows)
    pairs = (
        (discount, discount_in),
        (trace, trace_in),
        (dones, dones_in),
        (own, own_out),
        (rewards, rewards_out),
    )
    copies = [pltpu.make_async_copy(*pair, sems.at[k]) for k, pair in enumerate(pairs)]
    for copy in copies:
        copy.start()
    copies[0].wait()
    copies[1].wait()
    disc = to_column(discount_in[...], rows)
    lam = to_column(trace_in[...], rows)
    rate = disc * lam
    boot = disc * (1.0 - lam)
    consts_out[0] = rate
    consts_out[1] = (1.0 - lam) / lam
    copies[2].wait()
    scale = jnp.ones((rows, LANES), jnp.float32)
    saa = jnp.zeros((rows, LANES), jnp.float32)
    for j in reversed(range(tiles)):
        keep = 1.0 - dones_in[:, at(j)].astype(jnp.float32)
        boot_out[:, at(j)] = boot * keep
        a = rate * keep
        for k, step in enumerate(STEPS):
            inside = lane < LANES - step
            gates_out[k, :, at(j)] = jnp.where(inside, a, 0.0)
            a = jnp.where(inside, a * pltpu.roll(a, LANES - step, 1), a)
        head = spread(a[:, :1], rows)
        alpha = a * scale
        decay_out[:, at(j)] = a
        alpha_out[:, at(j)] = alpha
        heads_out[j] = head
        scale = head * scale
        saa += alpha * alpha
    consts_out[2] = scale
    consts_out[3] = spread(jnp.sum(saa, axis=1, keepdims=True), rows)
    copies[3].wait()
    copies[4].wait()


def local_kernel(
    rewards, own, *refs,
):
    members = lax.axis_size("member")
    others, (gates, decay, alpha, boot, heads, consts, scan_out, mean_out, stats_out) = (
        refs[: members - 1],
        refs[members - 1 :],
    )
    rows, moves = rewards.shape
    tiles = moves // LANES
    sub, lane = iotas(rows)
    block, blocks = lax.axis_index("tm"), lax.axis_size("tm")
    me = lax.axis_index("member")
    first = (lax.rem(lax.axis_index("games"), LANES // (blocks * SLOT)) * blocks + block) * SLOT

    def mean_of(parts):
        return sum(parts[1:], parts[0]) / members

    def guess_of(value):
        found = spread(value - rewards[:, moves - 1 : moves], rows) / rate
        return jnp.where(block == blocks - 1, 0.0, found)

    rate, ratio, slope, saa = consts[0], consts[1], consts[2], consts[3]
    lasts = [ref[:, moves - 1 : moves] for ref in (own, *others)]
    guess = guess_of(mean_of(lasts))
    guesses = [guess_of(last) for last in lasts]

    zero = jnp.zeros((rows, LANES), jnp.float32)
    carry, ahead = guess, zero
    suu, sua = zero, zero
    sqq, sqa = [zero] * members, [zero] * members
    for j in reversed(range(tiles)):
        parts = [ref[:, at(j)] for ref in (own, *others)]
        mean = mean_of(parts)
        mean_out[:, at(j)] = mean
        shifted = pltpu.roll(mean, LANES - 1, 1)
        following = jnp.where(lane == LANES - 1, ahead, shifted)
        ahead = shifted
        b = rewards[:, at(j)] + boot[:, at(j)] * following
        for k, step in enumerate(STEPS):
            b = b + gates[k, :, at(j)] * pltpu.roll(b, LANES - step, 1)
        result = b + decay[:, at(j)] * carry
        scan_out[:, at(j)] = result
        carry = spread(b[:, :1], rows) + heads[j] * carry
        weight = alpha[:, at(j)]
        u = result - mean
        suu += u * u
        sua += u * weight
        for m, part in enumerate(parts):
            q = part - result - weight * (guesses[m] - guess)
            sqq[m] += q * q
            sqa[m] += q * weight

    def total(x):
        return spread(jnp.sum(x, axis=1, keepdims=True), rows)

    entries = [carry + ratio * spread(mean_out[:, :1], rows), slope, guess]
    entries += [total(suu), total(sua), saa]
    stats = zero
    for k, entry in enumerate(entries):
        stats = jnp.where(lane == first + k, entry, stats)
    for m in range(members):
        at_lane = first + LOSSES + 3 * lax.rem(me + members - m, members)
        for k, entry in enumerate((guesses[m], total(sqq[m]), total(sqa[m]))):
            stats = jnp.where(lane == at_lane + k, entry, stats)
    stats_out[...] = stats


def chain(stats, blocks, picks):
    ahead = jnp.zeros_like(stats)
    for t in reversed(range(blocks)):
        moved = [pltpu.roll(stats, (LANES - t * SLOT - k) % LANES, 1) for k in range(picks)]
        eps = ahead - moved[2]
        yield t, ahead, eps, moved
        ahead = moved[0] + moved[1] * eps


def returns_kernel(
    moves_all, scan, alpha, mean, stats, returns_out, loss_out, raw_out, returns, loss, sems
):
    rows, moves = scan.shape
    tiles = moves // LANES
    sub, lane = iotas(rows)
    blocks, members = lax.axis_size("tm"), lax.axis_size("member")
    block, me = lax.axis_index("tm"), lax.axis_index("member")
    first = lax.rem(lax.axis_index("games"), LANES // (blocks * SLOT)) * blocks * SLOT
    zero = jnp.zeros((rows, LANES), jnp.float32)
    own_eps, own_loss = zero, zero
    for t, ahead, eps, moved in chain(stats[...], blocks, LOSSES + 3 * members):
        saa = moved[5]
        own_eps += jnp.where((lane == first) & (block == t), eps, 0.0)
        for m in range(members):
            guess, sqq, sqa = moved[LOSSES + 3 * m : LOSSES + 3 * m + 3]
            off = ahead - guess
            term = sqq + off * (off * saa - 2.0 * sqa)
            own_loss += jnp.where((lane == first) & (me == m), term, 0.0)
    eps = spread(jnp.sum(own_eps, axis=1, keepdims=True), rows)
    for j in range(tiles):
        result = scan[:, at(j)] + alpha[:, at(j)] * eps
        returns[:, at(j)] = result
        raw_out[:, at(j)] = result - mean[:, at(j)]
    column = spread(jnp.sum(own_loss, axis=1, keepdims=True), rows)
    loss_row = jnp.sum(jnp.where(lane == sub, column, 0.0), axis=0, keepdims=True)
    loss[...] = loss_row[:, :rows] / moves_all
    copies = [
        pltpu.make_async_copy(returns, returns_out, sems.at[0]),
        pltpu.make_async_copy(loss, loss_out, sems.at[1]),
    ]
    for copy in copies:
        copy.start()
    for copy in copies:
        copy.wait()


def scale_kernel(cells_all, raw, *refs):
    *stats, adv_out, adv, sems = refs
    rows, moves = raw.shape
    tiles = moves // LANES
    sub, lane = iotas(rows)
    blocks = lax.axis_size("tm")
    head = lax.rem(lane, blocks * SLOT) == 0
    squares = jnp.zeros((rows, LANES), jnp.float32)
    for ref in stats:
        for n in range(ref.shape[0]):
            for t, ahead, eps, moved in chain(ref[n], blocks, LOSSES):
                suu, sua, saa = moved[3:LOSSES]
                squares += jnp.where(head, suu + eps * (2.0 * sua + eps * saa), 0.0)
    total = jnp.sum(jnp.sum(squares, axis=1, keepdims=True), axis=0, keepdims=True)
    norm_scale = jnp.broadcast_to(lax.rsqrt(total / cells_all + 1e-06), (rows, LANES))
    for j in range(tiles):
        adv[:, at(j)] = raw[:, at(j)] * norm_scale
    copy = pltpu.make_async_copy(adv, adv_out, sems.at[0])
    copy.start()
    copy.wait()


def exchange(value, axis, bit):
    names = ("tm", "games", "member")
    sizes = [lax.axis_size(name) for name in names]
    pairs = []
    for t in range(sizes[0]):
        for g in range(sizes[1]):
            for m in range(sizes[2]):
                to = [t, g, (m + 1) % sizes[2]]
                to[names.index(axis)] ^= bit
                pairs.append(
                    ((t * sizes[1] + g) * sizes[2] + m, (to[0] * sizes[1] + to[1]) * sizes[2] + to[2])
                )
    return lax.ppermute(value, names, pairs)


def bits(count):
    return [1 << k for k in range(count.bit_length() - 1)]


def per_device(rewards, dones, values, discount, trace):
    members = lax.axis_size("member")
    blocks = lax.axis_size("tm")
    groups = lax.axis_size("games")
    own = values[0]
    rows, moves = own.shape
    tiles = moves // LANES
    others = [
        lax.ppermute(own, "member", [(m, (m + turn) % members) for m in range(members)])
        for turn in range(members - 1, 0, -1)
    ]

    def array(*shape):
        return jax.ShapeDtypeStruct(shape, jnp.float32)

    params = pltpu.CompilerParams(vmem_limit_bytes=VMEM_LIMIT)
    block = array(rows, moves)
    kept_rewards, kept_own, gates, decay, alpha, boot, heads, consts = pl.pallas_call(
        decay_kernel,
        out_shape=(
            block, block, array(len(STEPS), rows, moves), block, block, block,
            array(tiles, rows, LANES), array(4, rows, LANES),
        ),
        in_specs=[HBM] * 5,
        out_specs=(VMEM,) * 8,
        scratch_shapes=[
            pltpu.VMEM((rows, moves), jnp.int32),
            pltpu.VMEM((1, rows), jnp.float32),
            pltpu.VMEM((1, rows), jnp.float32),
            pltpu.SemaphoreType.DMA((5,)),
        ],
        compiler_params=params,
        cost_estimate=pl.CostEstimate(flops=4000000, bytes_accessed=2000000, transcendentals=0),
        name="decay_scan",
    )(
        *(
            pltpu.with_memory_space_constraint(x, pltpu.HBM)
            for x in (rewards, dones, own, discount[None], trace[None])
        )
    )
    scan, mean, stats = pl.pallas_call(
        local_kernel,
        out_shape=(block, block, array(rows, LANES)),
        in_specs=[VMEM] * (members + 7),
        out_specs=(VMEM,) * 3,
        compiler_params=params,
        name="local_scan",
    )(kept_rewards, kept_own, *others, gates, decay, alpha, boot, heads, consts)

    for bit in bits(blocks):
        stats = stats + exchange(stats, "tm", bit)
    moves_all = moves * blocks
    returns, loss, raw = pl.pallas_call(
        functools.partial(returns_kernel, float(moves_all)),
        out_shape=(block, array(1, rows), block),
        in_specs=[VMEM] * 4,
        out_specs=(HBM, HBM, VMEM),
        scratch_shapes=[
            pltpu.VMEM((rows, moves), jnp.float32),
            pltpu.VMEM((1, rows), jnp.float32),
            pltpu.SemaphoreType.DMA((2,)),
        ],
        compiler_params=params,
        cost_estimate=pl.CostEstimate(flops=2000000, bytes_accessed=1000000, transcendentals=0),
        name="write_returns",
    )(scan, alpha, mean, stats)
    packed = LANES // (blocks * SLOT)
    for bit in bits(min(groups, packed)):
        stats = stats + exchange(stats, "games", bit)
    stats = [stats[None]]
    for bit in bits(groups)[len(bits(packed)) :]:
        held = stats[0] if len(stats) == 1 else jnp.concatenate(stats)
        stats = [held, exchange(held, "games", bit)]
    advantages = pl.pallas_call(
        functools.partial(scale_kernel, float(moves_all * rows * groups)),
        out_shape=block,
        in_specs=[VMEM] * (1 + len(stats)),
        out_specs=HBM,
        scratch_shapes=[pltpu.VMEM((rows, moves), jnp.float32), pltpu.SemaphoreType.DMA((1,))],
        compiler_params=params,
        name="scale",
    )(raw, *stats)
    return returns, advantages, loss


def solution(mesh):
    return jax.shard_map(
        per_device,
        mesh=mesh,
        in_specs=(
            P("games", "tm"),
            P("games", "tm"),
            P("member", "games", "tm"),
            P("games"),
            P("games"),
        ),
        out_specs=(P("games", "tm"), P("games", "tm"), P("member", "games")),
        check_vma=False,
    )
```

time: 19.9 us -> 18.9 us (0.950)
  blocking collectives: 15.1 us -> 0 us
  starting transfers between devices: 0.56 us -> 9.42 us
  waiting for transfers between devices: 0.01 us -> 4.43 us
  Pallas kernels: 3.4 us -> 4.22 us
    all_to_all x1 -> x0, blocking collectives: 15.1 us -> none  [per_device(): stats = lax.all_to_all(stats, ('tm', 'games'), 0, 0, tiled=True)]
    ppermute x0 -> x4, starting transfers between devices: none -> 8.86 us  [exchange(): return lax.ppermute(value, names, pairs)]
    ppermute x0 -> x4, waiting for transfers between devices: none -> 4.43 us  [exchange(): return lax.ppermute(value, names, pairs)]
    pallas_call x2 -> x3, Pallas kernels: 1.75 us -> 2.57 us  [the longest x1 0.88 us: per_device(): pl.pallas_call(functools.partial(scale_kernel, float(moves_all * rows * g...]
  transfers between devices with their start and end apart: 1 -> 5, of which waited for: 0 -> 4; matrix products, arithmetic and copies ran while one was open for 0% -> 0% of each run, Pallas kernels for 8% -> 14%
where the time goes in v2:
time: 18.9 us; the launch traced here: 18.7 us
  starting transfers between devices  9.42 us (50%)
  waiting for transfers between devices  4.43 us (23%)
  Pallas kernels  4.22 us (22%)
  between operations  0.66 us (3%)
    ppermute x4, starting transfers between devices, exchange(): return lax.ppermute(value, names, pairs)  8.86 us
    ppermute x4, waiting for transfers between devices, exchange(): return lax.ppermute(value, names, pairs)  4.43 us
    pallas_call x1, Pallas kernels, per_device(): pl.pallas_call(decay_kernel, out_shape=(block, block, array(len(STEPS), r...  1.65 us
    pallas_call x1, Pallas kernels, per_device(): pl.pallas_call(functools.partial(scale_kernel, float(moves_all * rows * g...  0.88 us
    pallas_call x1, Pallas kernels, per_device(): pl.pallas_call(functools.partial(returns_kernel, float(moves_all)), out_s...  0.88 us
    pallas_call x1, Pallas kernels, per_device(): pl.pallas_call(local_kernel, out_shape=(block, block, array(rows, LANES))...  0.81 us
    ppermute x1, starting transfers between devices, per_device(): lax.ppermute(own, 'member', [(m, (m + turn) % members) for m in range(mem...  0.56 us
  transfers between devices with their start and end apart: 5, of which 4 were waited for; matrix products, arithmetic and copies ran while one was open for 0% of the time, Pallas kernels for 14%

profile of v2, /device:TPU:0, one launch (start us, length us, event | category | flops | bytes accessed | tf_op | source)
XLA Modules:
  0.0 18.7 jit_solution(16848754029204769944)
XLA Ops:
  0.6 0.6 %collective-permute-start = (f32[8,4096]{1,0:T(8,128)}, f32[8,4096]{1,0:T(8,128)S(1)}, u32[]{:S(2)}, u32[]{:S(2)}) collective-permute-start(f32[8,4096]{1,0:T(8,128)} %bitcast.5), channel_id=1, source_target_pairs={{0,1},{1,0},{2,3},{3,2},{4,5},{5,4},{6,7},{7,6},{8,9},{9,8},{10,11... | collective-permute-start | bytes 393224 | tf_op jit(solution)/shard_map/ppermute | solution.py:254
  1.2 1.7 %decay_scan.1 = (f32[8,4096]{1,0:T(8,128)S(1)}, f32[8,4096]{1,0:T(8,128)S(1)}, f32[7,8,4096]{2,1,0:T(8,128)S(1)}, f32[8,4096]{1,0:T(8,128)S(1)}, f32[8,4096]{1,0...) custom-call(f32[8,4096]{1,0:T(8,128)} %rewards.1, s32[8,4096]{1,0:T(8,128)} %dones.1, ...), custom_call_target="tpu_custom_call" | custom-call | flops 4000000 | bytes 2000000 | tf_op jit(solution)/shard_map/decay_scan/pallas_call | solution.py:263
  2.8 0.0 collective-permute-done.refs_0_
  2.9 0.8 %local_scan.1 = (f32[8,4096]{1,0:T(8,128)S(1)}, f32[8,4096]{1,0:T(8,128)S(1)}, f32[8,128]{1,0:T(8,128)S(1)}) custom-call(f32[8,4096]{1,0:T(8,128)S(1)} %get-tuple-element.17.rewards, f32[8,4096]{1,0:T(8,128)S(1)} %get-tuple-element.18.own, f32[8,4096]{1,0:T(8,128)S(1)} %collective-permute-done.refs_0_, f32[7,8,4096]{2,1,0:T(8,128)S(1)} %get-tuple-element.19.refs_1_, ...), custom_call_target="tpu_custom_call" | custom-call | tf_op jit(solution)/shard_map/local_scan/pallas_call | solution.py:286
  3.7 2.7 %collective-permute-start.1 = (f32[8,128]{1,0:T(8,128)S(1)}, f32[8,128]{1,0:T(8,128)S(1)}, u32[]{:S(2)}, u32[]{:S(2)}) collective-permute-start(f32[8,128]{1,0:T(8,128)S(1)} %get-tuple-element.27), channel_id=1, source_target_pairs={{0,9},{1,8},{2,11},{3,10},{4,13},{5,12},{6,15},{7,14},{8,1},{9,0},... | collective-permute-start | bytes 12296 | tf_op jit(solution)/shard_map/ppermute | solution.py:239
  6.3 1.3 %collective-permute-done.1 = f32[8,128]{1,0:T(8,128)S(1)} collective-permute-done((f32[8,128]{1,0:T(8,128)S(1)}, f32[8,128]{1,0:T(8,128)S(1)}, u32[]{:S(2)}, u32[]{:S(2)}) %collective-permute-start.1) | collective-permute-done | bytes 4128 | tf_op jit(solution)/shard_map/ppermute | solution.py:239
  7.7 1.7 %collective-permute-start.2 = (f32[8,128]{1,0:T(8,128)S(1)}, f32[8,128]{1,0:T(8,128)S(1)}, u32[]{:S(2)}, u32[]{:S(2)}) collective-permute-start(f32[8,128]{1,0:T(8,128)S(1)} %add.9), channel_id=1, source_target_pairs={{0,17},{1,16},{2,19},{3,18},{4,21},{5,20},{6,23},{7,22},{8,25},{9,... | collective-permute-start | bytes 12296 | tf_op jit(solution)/shard_map/ppermute | solution.py:239
  9.4 1.3 %collective-permute-done.2 = f32[8,128]{1,0:T(8,128)S(1)} collective-permute-done((f32[8,128]{1,0:T(8,128)S(1)}, f32[8,128]{1,0:T(8,128)S(1)}, u32[]{:S(2)}, u32[]{:S(2)}) %collective-permute-start.2) | collective-permute-done | bytes 4128 | tf_op jit(solution)/shard_map/ppermute | solution.py:239
  10.7 1.8 %collective-permute-start.3 = (f32[8,128]{1,0:T(8,128)S(1)}, f32[8,128]{1,0:T(8,128)S(1)}, u32[]{:S(2)}, u32[]{:S(2)}) collective-permute-start(f32[8,128]{1,0:T(8,128)S(1)} %add.10.stats), channel_id=1, source_target_pairs={{0,3},{1,2},{2,1},{3,0},{4,7},{5,6},{6,5},{7,4},{8,11},{9,10},{10,... | collective-permute-start | bytes 12296 | tf_op jit(solution)/shard_map/ppermute | solution.py:239
  12.5 1.3 %collective-permute-done.3 = f32[8,128]{1,0:T(8,128)S(1)} collective-permute-done((f32[8,128]{1,0:T(8,128)S(1)}, f32[8,128]{1,0:T(8,128)S(1)}, u32[]{:S(2)}, u32[]{:S(2)}) %collective-permute-start.3) | collective-permute-done | bytes 4128 | tf_op jit(solution)/shard_map/ppermute | solution.py:239
  13.8 2.7 %collective-permute-start.4 = (f32[1,8,128]{2,1,0:T(8,128)S(1)}, f32[1,8,128]{2,1,0:T(8,128)S(1)}, u32[]{:S(2)}, u32[]{:S(2)}) collective-permute-start(f32[1,8,128]{2,1,0:T(8,128)S(1)} %add_bitcast_fusion.refs_0_), channel_id=1, source_target_pairs={{0,5},{1,4},{2,7},{3,6},{4,1},{5,0},{6,3},{7,2},{8,13},{9,12},{10,... | collective-permute-start | bytes 12296 | tf_op jit(solution)/shard_map/ppermute | solution.py:239
  16.5 0.9 %write_returns.1 = (f32[8,4096]{1,0:T(8,128)}, f32[1,8]{1,0:T(1,128)}, f32[8,4096]{1,0:T(8,128)S(1)}) custom-call(f32[8,4096]{1,0:T(8,128)S(1)} %get-tuple-element.25.scan, f32[8,4096]{1,0:T(8,128)S(1)} %get-tuple-element.21.refs_3_.alpha, f32[8,4096]{1,0:T(8,128)S(1)} %get-tuple-element.26.mean, f32[8,128]{1,0:T(8,128)S(1)} %add.10.stats), custom_call_target="tpu_custom_call" | custom-call | flops 2000000 | bytes 1000000 | tf_op jit(solution)/shard_map/write_returns/pallas_call | solution.py:298
  17.4 0.4 %collective-permute-done.4.refs_1_ = f32[1,8,128]{2,1,0:T(8,128)S(1)} collective-permute-done((f32[1,8,128]{2,1,0:T(8,128)S(1)}, f32[1,8,128]{2,1,0:T(8,128)S(1)}, u32[]{:S(2)}, u32[]{:S(2)}) %collective-permute-start.4) | collective-permute-done | bytes 4128 | tf_op jit(solution)/shard_map/ppermute | solution.py:239
  17.9 0.9 %scale.1 = f32[8,4096]{1,0:T(8,128)} custom-call(f32[8,4096]{1,0:T(8,128)S(1)} %get-tuple-element.29.raw, f32[1,8,128]{2,1,0:T(8,128)S(1)} %add_bitcast_fusion.refs_0_, f32[1,8,128]{2,1,0:T(8,128)S(1)} %collective-permute-done.4.refs_1_), custom_call_target="tpu_custom_call" | custom-call | tf_op jit(solution)/shard_map/scale/pallas_call | solution.py:319
  (3 shorter events, 0.0 us)
Async XLA Ops:
  0.6 2.2 %collective-permute-start = (f32[8,4096]{1,0:T(8,128)}, f32[8,4096]{1,0:T(8,128)S(1)}, u32[]{:S(2)}, u32[]{:S(2)}) collective-permute-start(f32[8,4096]{1,0:T(8,128)} %bitcast.5), channel_id=1, source_target_pairs={{0,1},{1,0},{2,3},{3,2},{4,5},{5,4},{6,7},{7,6},{8,9},{9,8},{10,11... | collective-permute-start | bytes 393224 | tf_op jit(solution)/shard_map/ppermute | solution.py:254
  3.7 4.0 %collective-permute-start.1 = (f32[8,128]{1,0:T(8,128)S(1)}, f32[8,128]{1,0:T(8,128)S(1)}, u32[]{:S(2)}, u32[]{:S(2)}) collective-permute-start(f32[8,128]{1,0:T(8,128)S(1)} %get-tuple-element.27), channel_id=1, source_target_pairs={{0,9},{1,8},{2,11},{3,10},{4,13},{5,12},{6,15},{7,14},{8,1},{9,0},... | collective-permute-start | bytes 12296 | tf_op jit(solution)/shard_map/ppermute | solution.py:239
  7.7 3.1 %collective-permute-start.2 = (f32[8,128]{1,0:T(8,128)S(1)}, f32[8,128]{1,0:T(8,128)S(1)}, u32[]{:S(2)}, u32[]{:S(2)}) collective-permute-start(f32[8,128]{1,0:T(8,128)S(1)} %add.9), channel_id=1, source_target_pairs={{0,17},{1,16},{2,19},{3,18},{4,21},{5,20},{6,23},{7,22},{8,25},{9,... | collective-permute-start | bytes 12296 | tf_op jit(solution)/shard_map/ppermute | solution.py:239
  10.7 3.1 %collective-permute-start.3 = (f32[8,128]{1,0:T(8,128)S(1)}, f32[8,128]{1,0:T(8,128)S(1)}, u32[]{:S(2)}, u32[]{:S(2)}) collective-permute-start(f32[8,128]{1,0:T(8,128)S(1)} %add.10.stats), channel_id=1, source_target_pairs={{0,3},{1,2},{2,1},{3,0},{4,7},{5,6},{6,5},{7,4},{8,11},{9,10},{10,... | collective-permute-start | bytes 12296 | tf_op jit(solution)/shard_map/ppermute | solution.py:239
  13.8 4.0 %collective-permute-start.4 = (f32[1,8,128]{2,1,0:T(8,128)S(1)}, f32[1,8,128]{2,1,0:T(8,128)S(1)}, u32[]{:S(2)}, u32[]{:S(2)}) collective-permute-start(f32[1,8,128]{2,1,0:T(8,128)S(1)} %add_bitcast_fusion.refs_0_), channel_id=1, source_target_pairs={{0,5},{1,4},{2,7},{3,6},{4,1},{5,0},{6,3},{7,2},{8,13},{9,12},{10,... | collective-permute-start | bytes 12296 | tf_op jit(solution)/shard_map/ppermute | solution.py:239

commit v3 on v2

v3 whole, which is shorter than its diff:
```python
import functools

import jax
import jax.numpy as jnp
from jax import lax
from jax.experimental import pallas as pl
from jax.experimental.pallas import tpu as pltpu
from jax.sharding import PartitionSpec as P

LANES = 128
SUBLANES = 8
CHUNK = LANES // SUBLANES
PITCH = CHUNK + 1
DEPTH = SUBLANES * PITCH
SLOT = 16
GUESSES = 3
SUMS = 8
LOSSES = SUMS + 3
VMEM = pl.BlockSpec(memory_space=pltpu.VMEM)
HBM = pl.BlockSpec(memory_space=pltpu.HBM)
VMEM_LIMIT = 4 << 20


def iotas(rows):
    shape = (rows, LANES)
    return (
        lax.broadcasted_iota(jnp.int32, shape, 0),
        lax.broadcasted_iota(jnp.int32, shape, 1),
    )


def spread(column, rows):
    return jnp.broadcast_to(column, (rows, LANES))


def at(j):
    return slice(j * LANES, (j + 1) * LANES)


def turn(ref, block, tiles):
    flat = jnp.concatenate(tiles, axis=0).T
    for s in range(SUBLANES):
        start = block * DEPTH + s * PITCH
        ref[start : start + CHUNK, :] = flat[s * CHUNK : (s + 1) * CHUNK]


def chunk_rows(ref, block):
    starts = [block * DEPTH + s * PITCH for s in range(SUBLANES)]
    return [ref[start : start + CHUNK, :] for start in starts]


def strip(block, v):
    return pl.ds(block * DEPTH + v, SUBLANES, stride=PITCH)


def from_next(moved, edge, fill):
    following = moved[1:] + [fill]
    return [jnp.where(edge, far, near) for near, far in zip(moved, following)]


def next_chunk(blocks, rows, fill):
    sub, lane = iotas(SUBLANES)
    up = [pltpu.roll(x, SUBLANES - 1, 0) for x in blocks]
    across = from_next([pltpu.roll(x, LANES - rows, 1) for x in up], lane >= LANES - rows, fill)
    return [jnp.where(sub == SUBLANES - 1, far, near) for near, far in zip(up, across)]


def tree_sum(terms):
    while len(terms) > 1:
        odd = terms[-1:] if len(terms) % 2 else []
        terms = [x + y for x, y in zip(terms[::2], terms[1::2])] + odd
    return terms[0]


def product(terms):
    while len(terms) > 1:
        odd = terms[-1:] if len(terms) % 2 else []
        terms = [x * y for x, y in zip(terms[::2], terms[1::2])] + odd
    return terms[0]


def chunks_on(x):
    return [pltpu.roll(x, SUBLANES - k, 0) for k in range(1, SUBLANES)]


def tiles_on(x, rows):
    return [pltpu.roll(x, LANES - k * rows, 1) for k in range(1, LANES // rows)]


def spans(x, onward, place, count):
    one = jnp.ones_like(x)
    run, between = one, []
    for k in range(1, count):
        between.append(jnp.where(place + k < count, run, 0.0))
        run = run * onward[k - 1]
    after = product([jnp.where(place + k < count, onward[k - 1], 1.0) for k in range(1, count)])
    before = product([jnp.where(place >= k, onward[count - k - 1], 1.0) for k in range(1, count)])
    return between, after, before, x * run


def per_row(column, rows):
    sub, lane = iotas(rows)
    picked = jnp.where(lax.rem(lane, rows) == sub, column, 0.0)
    return jnp.broadcast_to(jnp.sum(picked, axis=0, keepdims=True), (SUBLANES, LANES))


def decay_kernel(
    rewards, dones, own, discount, trace,
    own_out, rewards_turned, own_turned, decay_out, reach_out, alpha_turned,
    chunk_out, tile_out, inside_out, after_out, consts_out, squares_out,
    rewards_in, dones_in, discount_in, trace_in, work, sems,
):
    rows, moves = dones_in.shape
    group = LANES // rows
    count = moves // (LANES * group)
    sub, lane = iotas(SUBLANES)
    pairs = (
        (discount, discount_in),
        (trace, trace_in),
        (dones, dones_in),
        (own, own_out),
        (rewards, rewards_in),
    )
    copies = [pltpu.make_async_copy(*pair, sems.at[k]) for k, pair in enumerate(pairs)]
    for copy in copies:
        copy.start()

    def across(row):
        row = jnp.pad(row, ((0, 0), (0, LANES - rows)))
        row = jnp.broadcast_to(row, (SUBLANES, LANES))
        return tree_sum([row] + tiles_on(row, rows))

    copies[0].wait()
    copies[1].wait()
    disc, lam = across(discount_in[...]), across(trace_in[...])
    rate = disc * lam
    consts_out[0] = rate
    consts_out[1] = (1.0 - lam) / lam
    copies[2].wait()
    for b in range(count):
        tiles = [dones_in[:, at(b * group + t)].astype(jnp.float32) for t in range(group)]
        turn(work, b, tiles)
    insides, lasts, befores, wholes = [], [], [], []
    for b in range(count):
        reach = None
        for v in reversed(range(CHUNK)):
            a = rate * (1.0 - work[strip(b, v), :])
            reach = a if reach is None else a * reach
            decay_out[b, v] = a
            reach_out[b, v] = reach
        between, inside, before, whole = spans(reach, chunks_on(reach), sub, SUBLANES)
        for k, gate in enumerate(between):
            chunk_out[b, k] = gate
        chunk_out[b, SUBLANES - 1] = before
        for k, gate in enumerate(chunks_on(before)):
            chunk_out[b, SUBLANES + k] = gate
        place = lane // rows
        between, last, before, whole = spans(whole, tiles_on(whole, rows), place, group)
        for k, gate in enumerate(between):
            tile_out[b, k] = gate
        tile_out[b, group - 1] = before
        for k, gate in enumerate(tiles_on(before, rows)):
            tile_out[b, group + k] = gate
        inside_out[b] = inside
        insides.append(inside)
        lasts.append(last)
        wholes.append(whole)
    squares = jnp.zeros((SUBLANES, LANES), jnp.float32)
    beyond = jnp.ones((SUBLANES, LANES), jnp.float32)
    for b in reversed(range(count)):
        after_out[b, 0] = lasts[b]
        after_out[b, 1] = wholes[b]
        after = insides[b] * lasts[b] * beyond
        after_out[b, 2] = after
        beyond = beyond * wholes[b]
        for v in range(CHUNK):
            alpha = reach_out[b, v] * after
            alpha_turned[strip(b, v), :] = alpha
            squares += alpha * alpha
            if b == 0 and v == 0:
                consts_out[2] = alpha
    squares_out[...] = squares
    copies[3].wait()
    copies[4].wait()
    for k, ref in ((3, rewards_in), (4, own_out)):
        consts_out[k] = per_row(spread(ref[:, moves - 1 : moves], rows), rows)
    for src, dst in ((own_out, own_turned), (rewards_in, rewards_turned)):
        for b in range(count):
            turn(dst, b, [src[:, at(b * group + t)] for t in range(group)])


def local_kernel(rewards, own, *refs):
    members = lax.axis_size("member")
    others, refs = refs[: members - 1], refs[members - 1 :]
    decay, reach, chunk_gates, tile_gates, insides, afters, consts, squares, *refs = refs
    scan_turned, stats_out, sums, folds, *works = refs
    rows, moves = others[0].shape
    group = LANES // rows
    count = moves // (LANES * group)
    sub, lane = iotas(SUBLANES)
    block, blocks = lax.axis_index("tm"), lax.axis_size("tm")
    me = lax.axis_index("member")
    first = (lax.rem(lax.axis_index("games"), LANES // (blocks * SLOT)) * blocks + block) * SLOT
    rate, ratio, slope, last_reward, last_own = (consts[k] for k in range(5))
    values = [own, *works]
    for b in range(count):
        for src, dst in zip(others, works):
            turn(dst, b, [src[:, at(b * group + t)] for t in range(group)])

    def mean_of(parts):
        return sum(parts[1:], parts[0]) / members

    def guess_of(value):
        return jnp.where(block == blocks - 1, 0.0, (value - last_reward) / rate)

    lasts = [last_own]
    lasts += [per_row(spread(ref[:, moves - 1 : moves], rows), rows) for ref in others]
    guess = guess_of(mean_of(lasts))
    guesses = [guess_of(last) for last in lasts]

    zero = jnp.zeros((SUBLANES, LANES), jnp.float32)

    def mean_at(b, v):
        return mean_of([ref[strip(b, v), :] for ref in values])

    followers = next_chunk([mean_at(b, 0) for b in range(count)], rows, zero)
    withins, tiles = [], []
    for b in range(count):
        following, total = followers[b], None
        for v in reversed(range(CHUNK)):
            a = decay[b, v]
            x = rewards[strip(b, v), :] + ratio * a * following
            following = mean_at(b, v)
            total = x if total is None else x + a * total
            sums[b, v] = total
        moved = chunks_on(total)
        withins.append(tree_sum([chunk_gates[b, k] * x for k, x in enumerate(moved)]))
        around = [total] + moved
        tiles.append(
            tree_sum([chunk_gates[b, SUBLANES - 1 + k] * x for k, x in enumerate(around)])
        )
    beyond = zero
    carries = [None] * count
    for b in reversed(range(count)):
        moved = tiles_on(tiles[b], rows)
        onward = tree_sum([tile_gates[b, k] * x for k, x in enumerate(moved)])
        onward = onward + afters[b, 0] * beyond
        carries[b] = withins[b] + insides[b] * onward + afters[b, 2] * guess
        if b:
            around = [tiles[b]] + moved
            whole = tree_sum([tile_gates[b, group - 1 + k] * x for k, x in enumerate(around)])
            beyond = whole + afters[b, 1] * beyond

    suu, sua = zero, zero
    sqq, sqa = [zero] * members, [zero] * members
    for b in range(count):
        carry, after = carries[b], afters[b, 2]
        own_carries = [carry + after * (own_guess - guess) for own_guess in guesses]
        part_ua, part_qa = zero, [zero] * members
        for v in range(CHUNK):
            weight = reach[b, v]
            partial = sums[b, v]
            result = partial + weight * carry
            scan_turned[strip(b, v), :] = result
            parts = [ref[strip(b, v), :] for ref in values]
            mean = mean_of(parts)
            if b == 0 and v == 0:
                head = result + ratio * mean
            u = result - mean
            suu += u * u
            part_ua += u * weight
            for m, part in enumerate(parts):
                q = part - partial - weight * own_carries[m]
                sqq[m] += q * q
                part_qa[m] += q * weight
        sua += part_ua * after
        for m in range(members):
            sqa[m] += part_qa[m] * after

    def by_member(entries, m):
        found = entries[0]
        for turn_of in range(1, members):
            found = jnp.where(lax.rem(me + turn_of, members) == m, entries[turn_of], found)
        return found

    held = jnp.where(sub == 0, head, zero)
    singles = [slope, guess] + [by_member(guesses, m) for m in range(members)]
    for k, entry in enumerate(singles):
        held = jnp.where(sub == 1 + k, jnp.broadcast_to(entry[:1], held.shape), held)
    held = jnp.where(lane < rows, held, 0.0)
    totals = [suu, sua, squares[...]]
    for m in range(members):
        totals += [by_member(sqq, m), by_member(sqa, m)]
    totals += [zero] * (SUBLANES - len(totals))
    for k, entry in enumerate(totals):
        folds[k * (SUBLANES + 1) : k * (SUBLANES + 1) + SUBLANES, :] = entry
    folded = tree_sum(
        [folds[pl.ds(s, SUBLANES, stride=SUBLANES + 1), :] for s in range(SUBLANES)]
    )
    flat = jnp.concatenate([held, folded], axis=0).T
    per_game = tree_sum([flat[t * rows : (t + 1) * rows] for t in range(group)])
    padded = jnp.pad(per_game, ((0, 0), (0, LANES - SLOT)))
    stats_out[...] = pltpu.roll(padded, first, 1)


def chain(stats, blocks, picks):
    ahead = jnp.zeros_like(stats)
    for t in reversed(range(blocks)):
        moved = [pltpu.roll(stats, (LANES - t * SLOT - k) % LANES, 1) for k in range(picks)]
        eps = ahead - moved[2]
        yield t, ahead, eps, moved
        ahead = moved[0] + moved[1] * eps


def returns_kernel(
    moves_all, scan, alpha, stats, *refs
):
    members = lax.axis_size("member")
    values, (returns_out, loss_out, raw_out, returns, loss, sems) = refs[:members], refs[members:]
    rows, moves = values[0].shape
    group = LANES // rows
    count = moves // (LANES * group)
    sub, lane = iotas(rows)
    blocks = lax.axis_size("tm")
    block, me = lax.axis_index("tm"), lax.axis_index("member")
    first = lax.rem(lax.axis_index("games"), LANES // (blocks * SLOT)) * blocks * SLOT
    zero = jnp.zeros((rows, LANES), jnp.float32)
    own_eps, own_loss = zero, zero
    for t, ahead, eps, moved in chain(stats[...], blocks, LOSSES + 2 * members):
        saa = moved[SUMS + 2]
        own_eps += jnp.where((lane == first) & (block == t), eps, 0.0)
        for m in range(members):
            sqq, sqa = moved[LOSSES + 2 * m : LOSSES + 2 * m + 2]
            guess = moved[GUESSES + m]
            off = ahead - guess
            term = sqq + off * (off * saa - 2.0 * sqa)
            own_loss += jnp.where((lane == first) & (me == m), term, 0.0)
    eps = spread(jnp.sum(own_eps, axis=1, keepdims=True), rows)
    eps = per_row(eps, rows)[:1]
    for b in range(count):
        pairs = zip(chunk_rows(scan, b), chunk_rows(alpha, b))
        flat = jnp.concatenate([part + weight * eps for part, weight in pairs], axis=0).T
        for t in range(group):
            j = b * group + t
            result = flat[t * rows : (t + 1) * rows]
            returns[:, at(j)] = result
            parts = [ref[:, at(j)] for ref in values]
            raw_out[:, at(j)] = result - sum(parts[1:], parts[0]) / members
    column = spread(jnp.sum(own_loss, axis=1, keepdims=True), rows)
    loss_row = jnp.sum(jnp.where(lane == sub, column, 0.0), axis=0, keepdims=True)
    loss[...] = loss_row[:, :rows] / moves_all
    copies = [
        pltpu.make_async_copy(returns, returns_out, sems.at[0]),
        pltpu.make_async_copy(loss, loss_out, sems.at[1]),
    ]
    for copy in copies:
        copy.start()
    for copy in copies:
        copy.wait()


def scale_kernel(cells_all, raw, *refs):
    *stats, adv_out, adv, sems = refs
    rows, moves = raw.shape
    tiles = moves // LANES
    sub, lane = iotas(rows)
    blocks = lax.axis_size("tm")
    head = lax.rem(lane, blocks * SLOT) == 0
    squares = jnp.zeros((rows, LANES), jnp.float32)
    for ref in stats:
        for n in range(ref.shape[0]):
            for t, ahead, eps, moved in chain(ref[n], blocks, LOSSES):
                suu, sua, saa = moved[SUMS:LOSSES]
                squares += jnp.where(head, suu + eps * (2.0 * sua + eps * saa), 0.0)
    total = jnp.sum(jnp.sum(squares, axis=1, keepdims=True), axis=0, keepdims=True)
    norm_scale = jnp.broadcast_to(lax.rsqrt(total / cells_all + 1e-06), (rows, LANES))
    for j in range(tiles):
        adv[:, at(j)] = raw[:, at(j)] * norm_scale
    copy = pltpu.make_async_copy(adv, adv_out, sems.at[0])
    copy.start()
    copy.wait()


def exchange(value, axis, bit):
    names = ("tm", "games", "member")
    sizes = [lax.axis_size(name) for name in names]
    pairs = []
    for t in range(sizes[0]):
        for g in range(sizes[1]):
            for m in range(sizes[2]):
                to = [t, g, (m + 1) % sizes[2]]
                to[names.index(axis)] ^= bit
                pairs.append(
                    ((t * sizes[1] + g) * sizes[2] + m, (to[0] * sizes[1] + to[1]) * sizes[2] + to[2])
                )
    return lax.ppermute(value, names, pairs)


def bits(count):
    return [1 << k for k in range(count.bit_length() - 1)]


def per_device(rewards, dones, values, discount, trace):
    members = lax.axis_size("member")
    blocks = lax.axis_size("tm")
    groups = lax.axis_size("games")
    own = values[0]
    rows, moves = own.shape
    others = [
        lax.ppermute(own, "member", [(m, (m + turn) % members) for m in range(members)])
        for turn in range(members - 1, 0, -1)
    ]

    def array(*shape):
        return jax.ShapeDtypeStruct(shape, jnp.float32)

    params = pltpu.CompilerParams(vmem_limit_bytes=VMEM_LIMIT)
    block = array(rows, moves)
    group = LANES // rows
    count = moves // (LANES * group)
    flat = array(count * DEPTH, LANES)
    strips = array(count, CHUNK, SUBLANES, LANES)
    row = pltpu.VMEM((1, rows), jnp.float32)
    kept_own, *kept = pl.pallas_call(
        decay_kernel,
        out_shape=(
            block, flat, flat, strips, strips, flat,
            array(count, 2 * SUBLANES - 1, SUBLANES, LANES),
            array(count, 2 * group - 1, SUBLANES, LANES),
            array(count, SUBLANES, LANES),
            array(count, 3, SUBLANES, LANES),
            array(5, SUBLANES, LANES),
            array(SUBLANES, LANES),
        ),
        in_specs=[HBM] * 5,
        out_specs=(VMEM,) * 12,
        scratch_shapes=[
            pltpu.VMEM((rows, moves), jnp.float32),
            pltpu.VMEM((rows, moves), jnp.int32),
            row,
            row,
            pltpu.VMEM((count * DEPTH, LANES), jnp.float32),
            pltpu.SemaphoreType.DMA((5,)),
        ],
        compiler_params=params,
        cost_estimate=pl.CostEstimate(flops=4000000, bytes_accessed=2000000, transcendentals=0),
        name="decay_scan",
    )(
        *(
            pltpu.with_memory_space_constraint(x, pltpu.HBM)
            for x in (rewards, dones, own, discount[None], trace[None])
        )
    )
    rewards_turned, own_turned, decay, reach, alpha, *gates = kept
    scan, stats = pl.pallas_call(
        local_kernel,
        out_shape=(flat, array(rows, LANES)),
        in_specs=[VMEM] * (members + 9),
        out_specs=(VMEM,) * 2,
        scratch_shapes=[
            pltpu.VMEM((count, CHUNK, SUBLANES, LANES), jnp.float32),
            pltpu.VMEM((SUBLANES * (SUBLANES + 1), LANES), jnp.float32),
        ]
        + [pltpu.VMEM((count * DEPTH, LANES), jnp.float32)] * (members - 1),
        compiler_params=params,
        name="local_scan",
    )(rewards_turned, own_turned, *others, decay, reach, *gates)

    for bit in bits(blocks):
        stats = stats + exchange(stats, "tm", bit)
    moves_all = moves * blocks
    returns, loss, raw = pl.pallas_call(
        functools.partial(returns_kernel, float(moves_all)),
        out_shape=(block, array(1, rows), block),
        in_specs=[VMEM] * (3 + members),
        out_specs=(HBM, HBM, VMEM),
        scratch_shapes=[
            pltpu.VMEM((rows, moves), jnp.float32),
            pltpu.VMEM((1, rows), jnp.float32),
            pltpu.SemaphoreType.DMA((2,)),
        ],
        compiler_params=params,
        cost_estimate=pl.CostEstimate(flops=2000000, bytes_accessed=1000000, transcendentals=0),
        name="write_returns",
    )(scan, alpha, stats, kept_own, *others)
    packed = LANES // (blocks * SLOT)
    for bit in bits(min(groups, packed)):
        stats = stats + exchange(stats, "games", bit)
    stats = [stats[None]]
    for bit in bits(groups)[len(bits(packed)) :]:
        held = stats[0] if len(stats) == 1 else jnp.concatenate(stats)
        stats = [held, exchange(held, "games", bit)]
    advantages = pl.pallas_call(
        functools.partial(scale_kernel, float(moves_all * rows * groups)),
        out_shape=block,
        in_specs=[VMEM] * (1 + len(stats)),
        out_specs=HBM,
        scratch_shapes=[pltpu.VMEM((rows, moves), jnp.float32), pltpu.SemaphoreType.DMA((1,))],
        compiler_params=params,
        name="scale",
    )(raw, *stats)
    return returns, advantages, loss


def solution(mesh):
    return jax.shard_map(
        per_device,
        mesh=mesh,
        in_specs=(
            P("games", "tm"),
            P("games", "tm"),
            P("member", "games", "tm"),
            P("games"),
            P("games"),
        ),
        out_specs=(P("games", "tm"), P("games", "tm"), P("member", "games")),
        check_vma=False,
    )
```

time: 18.9 us -> 18.5 us (0.979)
  Pallas kernels: 4.22 us -> 3.91 us
    pallas_call x2, Pallas kernels: 2.47 us -> 2.07 us  [the longest x1 1.48 us: per_device(): pl.pallas_call(decay_kernel, out_shape=(block, flat, flat, strips, strips...]
  transfers between devices with their start and end apart: 5 -> 5, of which waited for: 4 -> 4; matrix products, arithmetic and copies ran while one was open for 0% -> 0% of each run, Pallas kernels for 14% -> 13%
where the time goes in v3:
time: 18.5 us; the launch traced here: 18.3 us
  starting transfers between devices  9.37 us (51%)
  waiting for transfers between devices  4.35 us (24%)
  Pallas kernels  3.91 us (21%)
  between operations  0.66 us (4%)
    ppermute x4, starting transfers between devices, exchange(): return lax.ppermute(value, names, pairs)  8.81 us
    ppermute x4, waiting for transfers between devices, exchange(): return lax.ppermute(value, names, pairs)  4.34 us
    pallas_call x1, Pallas kernels, per_device(): pl.pallas_call(decay_kernel, out_shape=(block, flat, flat, strips, strips...  1.48 us
    pallas_call x1, Pallas kernels, per_device(): pl.pallas_call(functools.partial(returns_kernel, float(moves_all)), out_s...  0.96 us
    pallas_call x1, Pallas kernels, per_device(): pl.pallas_call(functools.partial(scale_kernel, float(moves_all * rows * g...  0.88 us
    pallas_call x1, Pallas kernels, per_device(): pl.pallas_call(local_kernel, out_shape=(flat, array(rows, LANES)), in_spe...  0.59 us
    ppermute x1, starting transfers between devices, per_device(): lax.ppermute(own, 'member', [(m, (m + turn) % members) for m in range(mem...  0.56 us
  transfers between devices with their start and end apart: 5, of which 4 were waited for; matrix products, arithmetic and copies ran while one was open for 0% of the time, Pallas kernels for 13%

profile of v3, /device:TPU:0, one launch (start us, length us, event | category | flops | bytes accessed | tf_op | source)
XLA Modules:
  0.0 18.3 jit_solution(14594914496059653019)
XLA Ops:
  0.6 0.6 %collective-permute-start = (f32[8,4096]{1,0:T(8,128)}, f32[8,4096]{1,0:T(8,128)S(1)}, u32[]{:S(2)}, u32[]{:S(2)}) collective-permute-start(f32[8,4096]{1,0:T(8,128)} %bitcast.5), channel_id=1, source_target_pairs={{0,1},{1,0},{2,3},{3,2},{4,5},{5,4},{6,7},{7,6},{8,9},{9,8},{10,11... | collective-permute-start | bytes 393224 | tf_op jit(solution)/shard_map/ppermute | solution.py:410
  1.2 1.5 %decay_scan.1 = (f32[8,4096]{1,0:T(8,128)S(1)}, f32[272,128]{1,0:T(8,128)S(1)}, f32[272,128]{1,0:T(8,128)S(1)}, f32[2,16,8,128]{3,2,1,0:T(8,128)S(1)}, f32[2,16,...) custom-call(f32[8,4096]{1,0:T(8,128)} %rewards.1, ...), custom_call_target="tpu_custom_call" | custom-call | flops 4000000 | bytes 2000000 | tf_op jit(solution)/shard_map/decay_scan/pallas_call | solution.py:424
  2.7 0.0 collective-permute-done.refs_0_.refs_1_
  2.7 0.6 %local_scan.1 = (f32[272,128]{1,0:T(8,128)S(1)}, f32[8,128]{1,0:T(8,128)S(1)}) custom-call(f32[272,128]{1,0:T(8,128)S(1)} %get-tuple-element.20.rewards, f32[272,128]{1,0:T(8,128)S(1)} %get-tuple-element.21.own, f32[8,4096]{1,0:T(8,128)S(1)} %collective-permute-done.refs_0_.refs_1_, f32[2,16,8,128]{3,2,1,0:T(8,128)S(1)} %get-tuple-element.22.refs_1_, ...), custom_call_target="tpu_custom_call" | custom-call | tf_op jit(solution)/shard_map/local_scan/pallas_call | solution.py:455
  3.3 2.6 %collective-permute-start.1 = (f32[8,128]{1,0:T(8,128)S(1)}, f32[8,128]{1,0:T(8,128)S(1)}, u32[]{:S(2)}, u32[]{:S(2)}) collective-permute-start(f32[8,128]{1,0:T(8,128)S(1)} %get-tuple-element.32), channel_id=1, source_target_pairs={{0,9},{1,8},{2,11},{3,10},{4,13},{5,12},{6,15},{7,14},{8,1},{9,0},... | collective-permute-start | bytes 12296 | tf_op jit(solution)/shard_map/ppermute | solution.py:396
  5.9 1.3 %collective-permute-done.1 = f32[8,128]{1,0:T(8,128)S(1)} collective-permute-done((f32[8,128]{1,0:T(8,128)S(1)}, f32[8,128]{1,0:T(8,128)S(1)}, u32[]{:S(2)}, u32[]{:S(2)}) %collective-permute-start.1) | collective-permute-done | bytes 4128 | tf_op jit(solution)/shard_map/ppermute | solution.py:396
  7.2 1.7 %collective-permute-start.2 = (f32[8,128]{1,0:T(8,128)S(1)}, f32[8,128]{1,0:T(8,128)S(1)}, u32[]{:S(2)}, u32[]{:S(2)}) collective-permute-start(f32[8,128]{1,0:T(8,128)S(1)} %add.9), channel_id=1, source_target_pairs={{0,17},{1,16},{2,19},{3,18},{4,21},{5,20},{6,23},{7,22},{8,25},{9,... | collective-permute-start | bytes 12296 | tf_op jit(solution)/shard_map/ppermute | solution.py:396
  8.9 1.3 %collective-permute-done.2 = f32[8,128]{1,0:T(8,128)S(1)} collective-permute-done((f32[8,128]{1,0:T(8,128)S(1)}, f32[8,128]{1,0:T(8,128)S(1)}, u32[]{:S(2)}, u32[]{:S(2)}) %collective-permute-start.2) | collective-permute-done | bytes 4128 | tf_op jit(solution)/shard_map/ppermute | solution.py:396
  10.3 1.8 %collective-permute-start.3 = (f32[8,128]{1,0:T(8,128)S(1)}, f32[8,128]{1,0:T(8,128)S(1)}, u32[]{:S(2)}, u32[]{:S(2)}) collective-permute-start(f32[8,128]{1,0:T(8,128)S(1)} %add.10.stats), channel_id=1, source_target_pairs={{0,3},{1,2},{2,1},{3,0},{4,7},{5,6},{6,5},{7,4},{8,11},{9,10},{10,... | collective-permute-start | bytes 12296 | tf_op jit(solution)/shard_map/ppermute | solution.py:396
  12.0 1.3 %collective-permute-done.3 = f32[8,128]{1,0:T(8,128)S(1)} collective-permute-done((f32[8,128]{1,0:T(8,128)S(1)}, f32[8,128]{1,0:T(8,128)S(1)}, u32[]{:S(2)}, u32[]{:S(2)}) %collective-permute-start.3) | collective-permute-done | bytes 4128 | tf_op jit(solution)/shard_map/ppermute | solution.py:396
  13.4 2.7 %collective-permute-start.4 = (f32[1,8,128]{2,1,0:T(8,128)S(1)}, f32[1,8,128]{2,1,0:T(8,128)S(1)}, u32[]{:S(2)}, u32[]{:S(2)}) collective-permute-start(f32[1,8,128]{2,1,0:T(8,128)S(1)} %add_bitcast_fusion.refs_0_), channel_id=1, source_target_pairs={{0,5},{1,4},{2,7},{3,6},{4,1},{5,0},{6,3},{7,2},{8,13},{9,12},{10,... | collective-permute-start | bytes 12296 | tf_op jit(solution)/shard_map/ppermute | solution.py:396
  16.1 1.0 %write_returns.1 = (f32[8,4096]{1,0:T(8,128)}, f32[1,8]{1,0:T(1,128)}, f32[8,4096]{1,0:T(8,128)S(1)}) custom-call(f32[272,128]{1,0:T(8,128)S(1)} %get-tuple-element.30.scan, f32[272,128]{1,0:T(8,128)S(1)} %get-tuple-element.31.alpha, f32[8,128]{1,0:T(8,128)S(1)} %add.10.stats, f32[8,4096]{1,0:T(8,128)S(1)} %get-tuple-element.33.refs_0_, ...), custom_call_target="tpu_custom_call" | custom-call | flops 2000000 | bytes 1000000 | tf_op jit(solution)/shard_map/write_returns/pallas_call | solution.py:472
  17.1 0.4 %collective-permute-done.4.refs_1_ = f32[1,8,128]{2,1,0:T(8,128)S(1)} collective-permute-done((f32[1,8,128]{2,1,0:T(8,128)S(1)}, f32[1,8,128]{2,1,0:T(8,128)S(1)}, u32[]{:S(2)}, u32[]{:S(2)}) %collective-permute-start.4) | collective-permute-done | bytes 4128 | tf_op jit(solution)/shard_map/ppermute | solution.py:396
  17.4 0.9 %scale.1 = f32[8,4096]{1,0:T(8,128)} custom-call(f32[8,4096]{1,0:T(8,128)S(1)} %get-tuple-element.35.raw, f32[1,8,128]{2,1,0:T(8,128)S(1)} %add_bitcast_fusion.refs_0_, f32[1,8,128]{2,1,0:T(8,128)S(1)} %collective-permute-done.4.refs_1_), custom_call_target="tpu_custom_call" | custom-call | tf_op jit(solution)/shard_map/scale/pallas_call | solution.py:493
  (3 shorter events, 0.0 us)
Async XLA Ops:
  0.6 2.0 %collective-permute-start = (f32[8,4096]{1,0:T(8,128)}, f32[8,4096]{1,0:T(8,128)S(1)}, u32[]{:S(2)}, u32[]{:S(2)}) collective-permute-start(f32[8,4096]{1,0:T(8,128)} %bitcast.5), channel_id=1, source_target_pairs={{0,1},{1,0},{2,3},{3,2},{4,5},{5,4},{6,7},{7,6},{8,9},{9,8},{10,11... | collective-permute-start | bytes 393224 | tf_op jit(solution)/shard_map/ppermute | solution.py:410
  3.3 3.9 %collective-permute-start.1 = (f32[8,128]{1,0:T(8,128)S(1)}, f32[8,128]{1,0:T(8,128)S(1)}, u32[]{:S(2)}, u32[]{:S(2)}) collective-permute-start(f32[8,128]{1,0:T(8,128)S(1)} %get-tuple-element.32), channel_id=1, source_target_pairs={{0,9},{1,8},{2,11},{3,10},{4,13},{5,12},{6,15},{7,14},{8,1},{9,0},... | collective-permute-start | bytes 12296 | tf_op jit(solution)/shard_map/ppermute | solution.py:396
  7.2 3.1 %collective-permute-start.2 = (f32[8,128]{1,0:T(8,128)S(1)}, f32[8,128]{1,0:T(8,128)S(1)}, u32[]{:S(2)}, u32[]{:S(2)}) collective-permute-start(f32[8,128]{1,0:T(8,128)S(1)} %add.9), channel_id=1, source_target_pairs={{0,17},{1,16},{2,19},{3,18},{4,21},{5,20},{6,23},{7,22},{8,25},{9,... | collective-permute-start | bytes 12296 | tf_op jit(solution)/shard_map/ppermute | solution.py:396
  10.3 3.1 %collective-permute-start.3 = (f32[8,128]{1,0:T(8,128)S(1)}, f32[8,128]{1,0:T(8,128)S(1)}, u32[]{:S(2)}, u32[]{:S(2)}) collective-permute-start(f32[8,128]{1,0:T(8,128)S(1)} %add.10.stats), channel_id=1, source_target_pairs={{0,3},{1,2},{2,1},{3,0},{4,7},{5,6},{6,5},{7,4},{8,11},{9,10},{10,... | collective-permute-start | bytes 12296 | tf_op jit(solution)/shard_map/ppermute | solution.py:396
  13.4 4.0 %collective-permute-start.4 = (f32[1,8,128]{2,1,0:T(8,128)S(1)}, f32[1,8,128]{2,1,0:T(8,128)S(1)}, u32[]{:S(2)}, u32[]{:S(2)}) collective-permute-start(f32[1,8,128]{2,1,0:T(8,128)S(1)} %add_bitcast_fusion.refs_0_), channel_id=1, source_target_pairs={{0,5},{1,4},{2,7},{3,6},{4,1},{5,0},{6,3},{7,2},{8,13},{9,12},{10,... | collective-permute-start | bytes 12296 | tf_op jit(solution)/shard_map/ppermute | solution.py:396

commit v4 on v3

--- a/solution.py
+++ b/solution.py
@@ -89,13 +89,19 @@
 
 def spans(x, onward, place, count):
     one = jnp.ones_like(x)
-    run, between = one, []
+    run, wrapped = one, one
+    between, after, parts = [], [], []
     for k in range(1, count):
-        between.append(jnp.where(place + k < count, run, 0.0))
-        run = run * onward[k - 1]
-    after = product([jnp.where(place + k < count, onward[k - 1], 1.0) for k in range(1, count)])
-    before = product([jnp.where(place >= k, onward[count - k - 1], 1.0) for k in range(1, count)])
-    return between, after, before, x * run
+        inside = place + k < count
+        value = onward[k - 1]
+        between.append(jnp.where(inside, run, 0.0))
+        after.append(jnp.where(inside, value, 1.0))
+        parts.append((inside, run, wrapped))
+        run = run * value
+        wrapped = wrapped * jnp.where(inside, 1.0, value)
+    here = x * wrapped
+    before = [wrapped] + [jnp.where(inside, here * ran, gone) for inside, ran, gone in parts]
+    return between, product(after), x * run, before
 
 
 def per_row(column, rows):
@@ -106,8 +112,8 @@
 
 def decay_kernel(
     rewards, dones, own, discount, trace,
-    own_out, rewards_turned, own_turned, decay_out, reach_out, alpha_turned,
-    chunk_out, tile_out, inside_out, after_out, consts_out, squares_out,
+    own_out, rewards_turned, own_turned, decay_out, reach_out,
+    powers_out, consts_out,
     rewards_in, dones_in, discount_in, trace_in, work, sems,
 ):
     rows, moves = dones_in.shape
@@ -136,53 +142,24 @@
     rate = disc * lam
     consts_out[0] = rate
     consts_out[1] = (1.0 - lam) / lam
-    copies[2].wait()
+    for copy in copies[2:]:
+        copy.wait()
     for b in range(count):
         tiles = [dones_in[:, at(b * group + t)].astype(jnp.float32) for t in range(group)]
         turn(work, b, tiles)
-    insides, lasts, befores, wholes = [], [], [], []
-    for b in range(count):
-        reach = None
+    powers = []
+    for b in range(count):
+        reach, power = None, jnp.zeros((SUBLANES, LANES), jnp.float32)
         for v in reversed(range(CHUNK)):
             a = rate * (1.0 - work[strip(b, v), :])
             reach = a if reach is None else a * reach
             decay_out[b, v] = a
             reach_out[b, v] = reach
-        between, inside, before, whole = spans(reach, chunks_on(reach), sub, SUBLANES)
-        for k, gate in enumerate(between):
-            chunk_out[b, k] = gate
-        chunk_out[b, SUBLANES - 1] = before
-        for k, gate in enumerate(chunks_on(before)):
-            chunk_out[b, SUBLANES + k] = gate
-        place = lane // rows
-        between, last, before, whole = spans(whole, tiles_on(whole, rows), place, group)
-        for k, gate in enumerate(between):
-            tile_out[b, k] = gate
-        tile_out[b, group - 1] = before
-        for k, gate in enumerate(tiles_on(before, rows)):
-            tile_out[b, group + k] = gate
-        inside_out[b] = inside
-        insides.append(inside)
-        lasts.append(last)
-        wholes.append(whole)
-    squares = jnp.zeros((SUBLANES, LANES), jnp.float32)
-    beyond = jnp.ones((SUBLANES, LANES), jnp.float32)
-    for b in reversed(range(count)):
-        after_out[b, 0] = lasts[b]
-        after_out[b, 1] = wholes[b]
-        after = insides[b] * lasts[b] * beyond
-        after_out[b, 2] = after
-        beyond = beyond * wholes[b]
-        for v in range(CHUNK):
-            alpha = reach_out[b, v] * after
-            alpha_turned[strip(b, v), :] = alpha
-            squares += alpha * alpha
-            if b == 0 and v == 0:
-                consts_out[2] = alpha
-    squares_out[...] = squares
-    copies[3].wait()
-    copies[4].wait()
-    for k, ref in ((3, rewards_in), (4, own_out)):
+            power += reach * reach
+        powers.append(power)
+    for b in range(count):
+        powers_out[b] = powers[b]
+    for k, ref in ((2, rewards_in), (3, own_out)):
         consts_out[k] = per_row(spread(ref[:, moves - 1 : moves], rows), rows)
     for src, dst in ((own_out, own_turned), (rewards_in, rewards_turned)):
         for b in range(count):
@@ -192,8 +169,7 @@
 def local_kernel(rewards, own, *refs):
     members = lax.axis_size("member")
     others, refs = refs[: members - 1], refs[members - 1 :]
-    decay, reach, chunk_gates, tile_gates, insides, afters, consts, squares, *refs = refs
-    scan_turned, stats_out, sums, folds, *works = refs
+    decay, reach, powers, consts, scan_out, after_out, stats_out, sums, folds, *works = refs
     rows, moves = others[0].shape
     group = LANES // rows
     count = moves // (LANES * group)
@@ -201,22 +177,42 @@
     block, blocks = lax.axis_index("tm"), lax.axis_size("tm")
     me = lax.axis_index("member")
     first = (lax.rem(lax.axis_index("games"), LANES // (blocks * SLOT)) * blocks + block) * SLOT
-    rate, ratio, slope, last_reward, last_own = (consts[k] for k in range(5))
+    rate, ratio, last_reward, last_own = (consts[k] for k in range(4))
     values = [own, *works]
     for b in range(count):
         for src, dst in zip(others, works):
             turn(dst, b, [src[:, at(b * group + t)] for t in range(group)])
 
+    chunk_gates, tile_gates = [], []
+    insides, lasts, wholes, afters = [], [], [], [None] * count
+    for b in range(count):
+        total = reach[b, 0]
+        between, inside, whole, before = spans(total, chunks_on(total), sub, SUBLANES)
+        chunk_gates.append((between, before))
+        insides.append(inside)
+        between, last, whole, before = spans(whole, tiles_on(whole, rows), lane // rows, group)
+        tile_gates.append((between, before))
+        lasts.append(last)
+        wholes.append(whole)
+    beyond = jnp.ones((SUBLANES, LANES), jnp.float32)
+    squares = jnp.zeros((SUBLANES, LANES), jnp.float32)
+    for b in reversed(range(count)):
+        afters[b] = insides[b] * lasts[b] * beyond
+        after_out[b] = afters[b]
+        beyond = beyond * wholes[b]
+        squares += powers[b] * (afters[b] * afters[b])
+    slope = reach[0, 0] * afters[0]
+
     def mean_of(parts):
         return sum(parts[1:], parts[0]) / members
 
     def guess_of(value):
         return jnp.where(block == blocks - 1, 0.0, (value - last_reward) / rate)
 
-    lasts = [last_own]
-    lasts += [per_row(spread(ref[:, moves - 1 : moves], rows), rows) for ref in others]
-    guess = guess_of(mean_of(lasts))
-    guesses = [guess_of(last) for last in lasts]
+    ends = [last_own]
+    ends += [per_row(spread(ref[:, moves - 1 : moves], rows), rows) for ref in others]
+    guess = guess_of(mean_of(ends))
+    guesses = [guess_of(end) for end in ends]
 
     zero = jnp.zeros((SUBLANES, LANES), jnp.float32)
 
@@ -234,34 +230,31 @@
             total = x if total is None else x + a * total
             sums[b, v] = total
         moved = chunks_on(total)
-        withins.append(tree_sum([chunk_gates[b, k] * x for k, x in enumerate(moved)]))
-        around = [total] + moved
-        tiles.append(
-            tree_sum([chunk_gates[b, SUBLANES - 1 + k] * x for k, x in enumerate(around)])
-        )
+        between, before = chunk_gates[b]
+        withins.append(tree_sum([gate * x for gate, x in zip(between, moved)]))
+        tiles.append(tree_sum([gate * x for gate, x in zip(before, [total] + moved)]))
     beyond = zero
     carries = [None] * count
     for b in reversed(range(count)):
         moved = tiles_on(tiles[b], rows)
-        onward = tree_sum([tile_gates[b, k] * x for k, x in enumerate(moved)])
-        onward = onward + afters[b, 0] * beyond
-        carries[b] = withins[b] + insides[b] * onward + afters[b, 2] * guess
+        between, before = tile_gates[b]
+        onward = tree_sum([gate * x for gate, x in zip(between, moved)]) + lasts[b] * beyond
+        carries[b] = withins[b] + insides[b] * onward + afters[b] * guess
         if b:
-            around = [tiles[b]] + moved
-            whole = tree_sum([tile_gates[b, group - 1 + k] * x for k, x in enumerate(around)])
-            beyond = whole + afters[b, 1] * beyond
+            whole = tree_sum([gate * x for gate, x in zip(before, [tiles[b]] + moved)])
+            beyond = whole + wholes[b] * beyond
 
     suu, sua = zero, zero
     sqq, sqa = [zero] * members, [zero] * members
     for b in range(count):
-        carry, after = carries[b], afters[b, 2]
+        carry, after = carries[b], afters[b]
         own_carries = [carry + after * (own_guess - guess) for own_guess in guesses]
         part_ua, part_qa = zero, [zero] * members
         for v in range(CHUNK):
             weight = reach[b, v]
             partial = sums[b, v]
             result = partial + weight * carry
-            scan_turned[strip(b, v), :] = result
+            scan_out[b, v] = result
             parts = [ref[strip(b, v), :] for ref in values]
             mean = mean_of(parts)
             if b == 0 and v == 0:
@@ -288,7 +281,7 @@
     for k, entry in enumerate(singles):
         held = jnp.where(sub == 1 + k, jnp.broadcast_to(entry[:1], held.shape), held)
     held = jnp.where(lane < rows, held, 0.0)
-    totals = [suu, sua, squares[...]]
+    totals = [suu, sua, squares]
     for m in range(members):
         totals += [by_member(sqq, m), by_member(sqa, m)]
     totals += [zero] * (SUBLANES - len(totals))
@@ -306,17 +299,27 @@
 def chain(stats, blocks, picks):
     ahead = jnp.zeros_like(stats)
     for t in reversed(range(blocks)):
-        moved = [pltpu.roll(stats, (LANES - t * SLOT - k) % LANES, 1) for k in range(picks)]
+        moved = {k: pltpu.roll(stats, (LANES - t * SLOT - k) % LANES, 1) for k in picks}
         eps = ahead - moved[2]
         yield t, ahead, eps, moved
         ahead = moved[0] + moved[1] * eps
 
 
+def squares_of(stats, blocks):
+    sub, lane = iotas(stats.shape[0])
+    found = jnp.zeros_like(stats)
+    for t, ahead, eps, moved in chain(stats, blocks, (0, 1, 2, SUMS, SUMS + 1, SUMS + 2)):
+        suu, sua, saa = (moved[SUMS + k] for k in range(3))
+        found += suu + eps * (2.0 * sua + eps * saa)
+    return jnp.where(lax.rem(lane, blocks * SLOT) == 0, found, 0.0)
+
+
 def returns_kernel(
-    moves_all, scan, alpha, stats, *refs
+    moves_all, scan, reach, afters, stats, *refs
 ):
     members = lax.axis_size("member")
-    values, (returns_out, loss_out, raw_out, returns, loss, sems) = refs[:members], refs[members:]
+    values, refs = refs[:members], refs[members:]
+    returns_out, loss_out, raw_out, squares_out, returns, loss, work, sems = refs
     rows, moves = values[0].shape
     group = LANES // rows
     count = moves // (LANES * group)
@@ -326,20 +329,23 @@
     first = lax.rem(lax.axis_index("games"), LANES // (blocks * SLOT)) * blocks * SLOT
     zero = jnp.zeros((rows, LANES), jnp.float32)
     own_eps, own_loss = zero, zero
-    for t, ahead, eps, moved in chain(stats[...], blocks, LOSSES + 2 * members):
+    squares_out[...] = squares_of(stats[...], blocks)
+    for t, ahead, eps, moved in chain(stats[...], blocks, range(LOSSES + 2 * members)):
         saa = moved[SUMS + 2]
         own_eps += jnp.where((lane == first) & (block == t), eps, 0.0)
         for m in range(members):
-            sqq, sqa = moved[LOSSES + 2 * m : LOSSES + 2 * m + 2]
+            sqq, sqa = moved[LOSSES + 2 * m], moved[LOSSES + 2 * m + 1]
             guess = moved[GUESSES + m]
             off = ahead - guess
             term = sqq + off * (off * saa - 2.0 * sqa)
             own_loss += jnp.where((lane == first) & (me == m), term, 0.0)
     eps = spread(jnp.sum(own_eps, axis=1, keepdims=True), rows)
-    eps = per_row(eps, rows)[:1]
-    for b in range(count):
-        pairs = zip(chunk_rows(scan, b), chunk_rows(alpha, b))
-        flat = jnp.concatenate([part + weight * eps for part, weight in pairs], axis=0).T
+    eps = per_row(eps, rows)
+    for b in range(count):
+        error = afters[b] * eps
+        for v in range(CHUNK):
+            work[strip(b, v), :] = scan[b, v] + reach[b, v] * error
+        flat = jnp.concatenate(chunk_rows(work, b), axis=0).T
         for t in range(group):
             j = b * group + t
             result = flat[t * rows : (t + 1) * rows]
@@ -359,21 +365,18 @@
         copy.wait()
 
 
-def scale_kernel(cells_all, raw, *refs):
-    *stats, adv_out, adv, sems = refs
+def scale_kernel(cells_all, raw, squares, *refs):
+    *stats, adv_out, adv, rows_in, sems = refs
     rows, moves = raw.shape
     tiles = moves // LANES
-    sub, lane = iotas(rows)
-    blocks = lax.axis_size("tm")
-    head = lax.rem(lane, blocks * SLOT) == 0
-    squares = jnp.zeros((rows, LANES), jnp.float32)
+    found = squares[...]
     for ref in stats:
         for n in range(ref.shape[0]):
-            for t, ahead, eps, moved in chain(ref[n], blocks, LOSSES):
-                suu, sua, saa = moved[SUMS:LOSSES]
-                squares += jnp.where(head, suu + eps * (2.0 * sua + eps * saa), 0.0)
-    total = jnp.sum(jnp.sum(squares, axis=1, keepdims=True), axis=0, keepdims=True)
-    norm_scale = jnp.broadcast_to(lax.rsqrt(total / cells_all + 1e-06), (rows, LANES))
+            found += squares_of(ref[n], lax.axis_size("tm"))
+    rows_in[...] = found
+    found = tree_sum([jnp.broadcast_to(rows_in[s : s + 1, :], found.shape) for s in range(rows)])
+    total = spread(jnp.sum(found, axis=1, keepdims=True), rows)
+    norm_scale = lax.rsqrt(total / cells_all + 1e-06)
     for j in range(tiles):
         adv[:, at(j)] = raw[:, at(j)] * norm_scale
     copy = pltpu.make_async_copy(adv, adv_out, sems.at[0])
@@ -424,16 +427,12 @@
     kept_own, *kept = pl.pallas_call(
         decay_kernel,
         out_shape=(
-            block, flat, flat, strips, strips, flat,
-            array(count, 2 * SUBLANES - 1, SUBLANES, LANES),
-            array(count, 2 * group - 1, SUBLANES, LANES),
+            block, flat, flat, strips, strips,
             array(count, SUBLANES, LANES),
-            array(count, 3, SUBLANES, LANES),
-            array(5, SUBLANES, LANES),
-            array(SUBLANES, LANES),
+            array(4, SUBLANES, LANES),
         ),
         in_specs=[HBM] * 5,
-        out_specs=(VMEM,) * 12,
+        out_specs=(VMEM,) * 7,
         scratch_shapes=[
             pltpu.VMEM((rows, moves), jnp.float32),
             pltpu.VMEM((rows, moves), jnp.int32),
@@ -451,12 +450,12 @@
             for x in (rewards, dones, own, discount[None], trace[None])
         )
     )
-    rewards_turned, own_turned, decay, reach, alpha, *gates = kept
-    scan, stats = pl.pallas_call(
+    rewards_turned, own_turned, decay, reach, powers, consts = kept
+    scan, afters, stats = pl.pallas_call(
         local_kernel,
-        out_shape=(flat, array(rows, LANES)),
-        in_specs=[VMEM] * (members + 9),
-        out_specs=(VMEM,) * 2,
+        out_shape=(strips, array(count, SUBLANES, LANES), array(rows, LANES)),
+        in_specs=[VMEM] * (members + 5),
+        out_specs=(VMEM,) * 3,
         scratch_shapes=[
             pltpu.VMEM((count, CHUNK, SUBLANES, LANES), jnp.float32),
             pltpu.VMEM((SUBLANES * (SUBLANES + 1), LANES), jnp.float32),
@@ -464,41 +463,47 @@
         + [pltpu.VMEM((count * DEPTH, LANES), jnp.float32)] * (members - 1),
         compiler_params=params,
         name="local_scan",
-    )(rewards_turned, own_turned, *others, decay, reach, *gates)
+    )(rewards_turned, own_turned, *others, decay, reach, powers, consts)
 
     for bit in bits(blocks):
         stats = stats + exchange(stats, "tm", bit)
+    packed = LANES // (blocks * SLOT)
+    for bit in bits(min(groups, packed)):
+        stats = stats + exchange(stats, "games", bit)
+    held, received = stats[None], []
+    for bit in bits(groups)[len(bits(packed)) :]:
+        if received:
+            held = jnp.concatenate([held, received[-1]])
+        received.append(exchange(held, "games", bit))
     moves_all = moves * blocks
-    returns, loss, raw = pl.pallas_call(
+    returns, loss, raw, squares = pl.pallas_call(
         functools.partial(returns_kernel, float(moves_all)),
-        out_shape=(block, array(1, rows), block),
-        in_specs=[VMEM] * (3 + members),
-        out_specs=(HBM, HBM, VMEM),
+        out_shape=(block, array(1, rows), block, array(rows, LANES)),
+        in_specs=[VMEM] * (4 + members),
+        out_specs=(HBM, HBM, VMEM, VMEM),
         scratch_shapes=[
             pltpu.VMEM((rows, moves), jnp.float32),
             pltpu.VMEM((1, rows), jnp.float32),
+            pltpu.VMEM((count * DEPTH, LANES), jnp.float32),
             pltpu.SemaphoreType.DMA((2,)),
         ],
         compiler_params=params,
         cost_estimate=pl.CostEstimate(flops=2000000, bytes_accessed=1000000, transcendentals=0),
         name="write_returns",
-    )(scan, alpha, stats, kept_own, *others)
-    packed = LANES // (blocks * SLOT)
-    for bit in bits(min(groups, packed)):
-        stats = stats + exchange(stats, "games", bit)
-    stats = [stats[None]]
-    for bit in bits(groups)[len(bits(packed)) :]:
-        held = stats[0] if len(stats) == 1 else jnp.concatenate(stats)
-        stats = [held, exchange(held, "games", bit)]
+    )(scan, reach, afters, stats, kept_own, *others)
     advantages = pl.pallas_call(
         functools.partial(scale_kernel, float(moves_all * rows * groups)),
         out_shape=block,
-        in_specs=[VMEM] * (1 + len(stats)),
+        in_specs=[VMEM] * (2 + len(received)),
         out_specs=HBM,
-        scratch_shapes=[pltpu.VMEM((rows, moves), jnp.float32), pltpu.SemaphoreType.DMA((1,))],
+        scratch_shapes=[
+            pltpu.VMEM((rows, moves), jnp.float32),
+            pltpu.VMEM((rows, LANES), jnp.float32),
+            pltpu.SemaphoreType.DMA((1,)),
+        ],
         compiler_params=params,
         name="scale",
-    )(raw, *stats)
+    )(raw, squares, *received)
     return returns, advantages, loss
 
 

time: 18.5 us -> 18.3 us (0.989)
  Pallas kernels: 3.91 us -> 3.72 us
  transfers between devices with their start and end apart: 5 -> 5, of which waited for: 4 -> 4; matrix products, arithmetic and copies ran while one was open for 0% -> 0% of each run, Pallas kernels for 13% -> 12%
where the time goes in v4:
time: 18.3 us; the launch traced here: 18.1 us
  starting transfers between devices  9.37 us (51%)
  waiting for transfers between devices  4.35 us (24%)
  Pallas kernels  3.72 us (20%)
  between operations  0.66 us (4%)
    ppermute x4, starting transfers between devices, exchange(): return lax.ppermute(value, names, pairs)  8.81 us
    ppermute x4, waiting for transfers between devices, exchange(): return lax.ppermute(value, names, pairs)  4.35 us
    pallas_call x1, Pallas kernels, per_device(): pl.pallas_call(decay_kernel, out_shape=(block, flat, flat, strips, strips...  1.3 us
    pallas_call x1, Pallas kernels, per_device(): pl.pallas_call(functools.partial(returns_kernel, float(moves_all)), out_s...  0.96 us
    pallas_call x1, Pallas kernels, per_device(): pl.pallas_call(functools.partial(scale_kernel, float(moves_all * rows * g...  0.86 us
    pallas_call x1, Pallas kernels, per_device(): pl.pallas_call(local_kernel, out_shape=(strips, array(count, SUBLANES, LA...  0.61 us
    ppermute x1, starting transfers between devices, per_device(): lax.ppermute(own, 'member', [(m, (m + turn) % members) for m in range(mem...  0.56 us
  transfers between devices with their start and end apart: 5, of which 4 were waited for; matrix products, arithmetic and copies ran while one was open for 0% of the time, Pallas kernels for 12%

profile of v4, /device:TPU:0, one launch (start us, length us, event | category | flops | bytes accessed | tf_op | source)
XLA Modules:
  0.0 18.1 jit_solution(10418001699036604813)
XLA Ops:
  0.6 0.6 %collective-permute-start = (f32[8,4096]{1,0:T(8,128)}, f32[8,4096]{1,0:T(8,128)S(1)}, u32[]{:S(2)}, u32[]{:S(2)}) collective-permute-start(f32[8,4096]{1,0:T(8,128)} %bitcast.5), channel_id=1, source_target_pairs={{0,1},{1,0},{2,3},{3,2},{4,5},{5,4},{6,7},{7,6},{8,9},{9,8},{10,11... | collective-permute-start | bytes 393224 | tf_op jit(solution)/shard_map/ppermute | solution.py:413
  1.2 1.3 %decay_scan.1 = (f32[8,4096]{1,0:T(8,128)S(1)}, f32[272,128]{1,0:T(8,128)S(1)}, f32[272,128]{1,0:T(8,128)S(1)}, f32[2,16,8,128]{3,2,1,0:T(8,128)S(1)}, f32[2,16,...) custom-call(f32[8,4096]{1,0:T(8,128)} %rewards.1, s32[8,4096]{1,0:T(8,128)} %dones.1, ...), custom_call_target="tpu_custom_call" | custom-call | flops 4000000 | bytes 2000000 | tf_op jit(solution)/shard_map/decay_scan/pallas_call | solution.py:427
  2.5 0.0 collective-permute-done.refs_0_.refs_1_
  2.5 0.6 %local_scan.1 = (f32[2,16,8,128]{3,2,1,0:T(8,128)S(1)}, f32[2,8,128]{2,1,0:T(8,128)S(1)}, f32[8,128]{1,0:T(8,128)S(1)}) custom-call(f32[272,128]{1,0:T(8,128)S(1)} %get-tuple-element.17.rewards, f32[272,128]{1,0:T(8,128)S(1)} %get-tuple-element.18.own, f32[8,4096]{1,0:T(8,128)S(1)} %collective-permute-done.refs_0_.refs_1_, ...), custom_call_target="tpu_custom_call" | custom-call | tf_op jit(solution)/shard_map/local_scan/pallas_call | solution.py:454
  3.1 2.6 %collective-permute-start.1 = (f32[8,128]{1,0:T(8,128)S(1)}, f32[8,128]{1,0:T(8,128)S(1)}, u32[]{:S(2)}, u32[]{:S(2)}) collective-permute-start(f32[8,128]{1,0:T(8,128)S(1)} %get-tuple-element.25), channel_id=1, source_target_pairs={{0,9},{1,8},{2,11},{3,10},{4,13},{5,12},{6,15},{7,14},{8,1},{9,0},... | collective-permute-start | bytes 12296 | tf_op jit(solution)/shard_map/ppermute | solution.py:399
  5.7 1.3 %collective-permute-done.1 = f32[8,128]{1,0:T(8,128)S(1)} collective-permute-done((f32[8,128]{1,0:T(8,128)S(1)}, f32[8,128]{1,0:T(8,128)S(1)}, u32[]{:S(2)}, u32[]{:S(2)}) %collective-permute-start.1) | collective-permute-done | bytes 4128 | tf_op jit(solution)/shard_map/ppermute | solution.py:399
  7.0 1.7 %collective-permute-start.2 = (f32[8,128]{1,0:T(8,128)S(1)}, f32[8,128]{1,0:T(8,128)S(1)}, u32[]{:S(2)}, u32[]{:S(2)}) collective-permute-start(f32[8,128]{1,0:T(8,128)S(1)} %add.9), channel_id=1, source_target_pairs={{0,17},{1,16},{2,19},{3,18},{4,21},{5,20},{6,23},{7,22},{8,25},{9,... | collective-permute-start | bytes 12296 | tf_op jit(solution)/shard_map/ppermute | solution.py:399
  8.8 1.3 %collective-permute-done.2 = f32[8,128]{1,0:T(8,128)S(1)} collective-permute-done((f32[8,128]{1,0:T(8,128)S(1)}, f32[8,128]{1,0:T(8,128)S(1)}, u32[]{:S(2)}, u32[]{:S(2)}) %collective-permute-start.2) | collective-permute-done | bytes 4128 | tf_op jit(solution)/shard_map/ppermute | solution.py:399
  10.1 1.8 %collective-permute-start.3 = (f32[8,128]{1,0:T(8,128)S(1)}, f32[8,128]{1,0:T(8,128)S(1)}, u32[]{:S(2)}, u32[]{:S(2)}) collective-permute-start(f32[8,128]{1,0:T(8,128)S(1)} %add.10), channel_id=1, source_target_pairs={{0,3},{1,2},{2,1},{3,0},{4,7},{5,6},{6,5},{7,4},{8,11},{9,10},{10,... | collective-permute-start | bytes 12296 | tf_op jit(solution)/shard_map/ppermute | solution.py:399
  11.9 1.3 %collective-permute-done.3 = f32[8,128]{1,0:T(8,128)S(1)} collective-permute-done((f32[8,128]{1,0:T(8,128)S(1)}, f32[8,128]{1,0:T(8,128)S(1)}, u32[]{:S(2)}, u32[]{:S(2)}) %collective-permute-start.3) | collective-permute-done | bytes 4128 | tf_op jit(solution)/shard_map/ppermute | solution.py:399
  13.2 2.7 %collective-permute-start.4 = (f32[1,8,128]{2,1,0:T(8,128)S(1)}, f32[1,8,128]{2,1,0:T(8,128)S(1)}, u32[]{:S(2)}, u32[]{:S(2)}) collective-permute-start(f32[1,8,128]{2,1,0:T(8,128)S(1)} %bitcast.4), channel_id=1, source_target_pairs={{0,5},{1,4},{2,7},{3,6},{4,1},{5,0},{6,3},{7,2},{8,13},{9,12},{10,... | collective-permute-start | bytes 12296 | tf_op jit(solution)/shard_map/ppermute | solution.py:399
  15.9 1.0 %write_returns.1 = (f32[8,4096]{1,0:T(8,128)}, f32[1,8]{1,0:T(1,128)}, f32[8,4096]{1,0:T(8,128)S(1)}, f32[8,128]{1,0:T(8,128)S(1)}) custom-call(f32[2,16,8,128]{3,2,1,0:T(8,128)S(1)} %get-tuple-element.23.scan, f32[2,16,8,128]{3,2,1,0:T(8,128)S(1)} %get-tuple-element.20.refs_2_.reach, f32[2,8,128]{2,1,0:T(8,128)S(1)} %get-tuple-element.24.afters, ...), custom_call_target="tpu_custom_call" | custom-call | flops 2000000 | bytes 1000000 | tf_op jit(solution)/shard_map/write_returns/pallas_call | solution.py:479
  16.9 0.4 %collective-permute-done.4.refs_0_ = f32[1,8,128]{2,1,0:T(8,128)S(1)} collective-permute-done((f32[1,8,128]{2,1,0:T(8,128)S(1)}, f32[1,8,128]{2,1,0:T(8,128)S(1)}, u32[]{:S(2)}, u32[]{:S(2)}) %collective-permute-start.4) | collective-permute-done | bytes 4128 | tf_op jit(solution)/shard_map/ppermute | solution.py:399
  17.3 0.9 %scale.1 = f32[8,4096]{1,0:T(8,128)} custom-call(f32[8,4096]{1,0:T(8,128)S(1)} %get-tuple-element.28.raw, f32[8,128]{1,0:T(8,128)S(1)} %get-tuple-element.29.squares, f32[1,8,128]{2,1,0:T(8,128)S(1)} %collective-permute-done.4.refs_0_), custom_call_target="tpu_custom_call" | custom-call | tf_op jit(solution)/shard_map/scale/pallas_call | solution.py:494
  (3 shorter events, 0.0 us)
Async XLA Ops:
  0.6 1.9 %collective-permute-start = (f32[8,4096]{1,0:T(8,128)}, f32[8,4096]{1,0:T(8,128)S(1)}, u32[]{:S(2)}, u32[]{:S(2)}) collective-permute-start(f32[8,4096]{1,0:T(8,128)} %bitcast.5), channel_id=1, source_target_pairs={{0,1},{1,0},{2,3},{3,2},{4,5},{5,4},{6,7},{7,6},{8,9},{9,8},{10,11... | collective-permute-start | bytes 393224 | tf_op jit(solution)/shard_map/ppermute | solution.py:413
  3.1 3.9 %collective-permute-start.1 = (f32[8,128]{1,0:T(8,128)S(1)}, f32[8,128]{1,0:T(8,128)S(1)}, u32[]{:S(2)}, u32[]{:S(2)}) collective-permute-start(f32[8,128]{1,0:T(8,128)S(1)} %get-tuple-element.25), channel_id=1, source_target_pairs={{0,9},{1,8},{2,11},{3,10},{4,13},{5,12},{6,15},{7,14},{8,1},{9,0},... | collective-permute-start | bytes 12296 | tf_op jit(solution)/shard_map/ppermute | solution.py:399
  7.0 3.1 %collective-permute-start.2 = (f32[8,128]{1,0:T(8,128)S(1)}, f32[8,128]{1,0:T(8,128)S(1)}, u32[]{:S(2)}, u32[]{:S(2)}) collective-permute-start(f32[8,128]{1,0:T(8,128)S(1)} %add.9), channel_id=1, source_target_pairs={{0,17},{1,16},{2,19},{3,18},{4,21},{5,20},{6,23},{7,22},{8,25},{9,... | collective-permute-start | bytes 12296 | tf_op jit(solution)/shard_map/ppermute | solution.py:399
  10.1 3.1 %collective-permute-start.3 = (f32[8,128]{1,0:T(8,128)S(1)}, f32[8,128]{1,0:T(8,128)S(1)}, u32[]{:S(2)}, u32[]{:S(2)}) collective-permute-start(f32[8,128]{1,0:T(8,128)S(1)} %add.10), channel_id=1, source_target_pairs={{0,3},{1,2},{2,1},{3,0},{4,7},{5,6},{6,5},{7,4},{8,11},{9,10},{10,... | collective-permute-start | bytes 12296 | tf_op jit(solution)/shard_map/ppermute | solution.py:399
  13.2 4.0 %collective-permute-start.4 = (f32[1,8,128]{2,1,0:T(8,128)S(1)}, f32[1,8,128]{2,1,0:T(8,128)S(1)}, u32[]{:S(2)}, u32[]{:S(2)}) collective-permute-start(f32[1,8,128]{2,1,0:T(8,128)S(1)} %bitcast.4), channel_id=1, source_target_pairs={{0,5},{1,4},{2,7},{3,6},{4,1},{5,0},{6,3},{7,2},{8,13},{9,12},{10,... | collective-permute-start | bytes 12296 | tf_op jit(solution)/shard_map/ppermute | solution.py:399

commit v5 on v4

--- a/solution.py
+++ b/solution.py
@@ -90,18 +90,17 @@
 def spans(x, onward, place, count):
     one = jnp.ones_like(x)
     run, wrapped = one, one
-    between, after, parts = [], [], []
+    between, parts = [], []
     for k in range(1, count):
         inside = place + k < count
         value = onward[k - 1]
         between.append(jnp.where(inside, run, 0.0))
-        after.append(jnp.where(inside, value, 1.0))
         parts.append((inside, run, wrapped))
-        run = run * value
+        run = run * jnp.where(inside, value, 1.0)
         wrapped = wrapped * jnp.where(inside, 1.0, value)
     here = x * wrapped
     before = [wrapped] + [jnp.where(inside, here * ran, gone) for inside, ran, gone in parts]
-    return between, product(after), x * run, before
+    return between, run, here * run, before
 
 
 def per_row(column, rows):
@@ -169,7 +168,7 @@
 def local_kernel(rewards, own, *refs):
     members = lax.axis_size("member")
     others, refs = refs[: members - 1], refs[members - 1 :]
-    decay, reach, powers, consts, scan_out, after_out, stats_out, sums, folds, *works = refs
+    decay, reach, powers, consts, sums, carry_out, after_out, stats_out, folds, *works = refs
     rows, moves = others[0].shape
     group = LANES // rows
     count = moves // (LANES * group)
@@ -244,31 +243,27 @@
             whole = tree_sum([gate * x for gate, x in zip(before, [tiles[b]] + moved)])
             beyond = whole + wholes[b] * beyond
 
-    suu, sua = zero, zero
+    head = sums[0, 0] + reach[0, 0] * carries[0] + ratio * mean_at(0, 0)
+    total = zero
     sqq, sqa = [zero] * members, [zero] * members
     for b in range(count):
         carry, after = carries[b], afters[b]
+        carry_out[b] = carry
         own_carries = [carry + after * (own_guess - guess) for own_guess in guesses]
-        part_ua, part_qa = zero, [zero] * members
+        part_qa = [zero] * members
         for v in range(CHUNK):
-            weight = reach[b, v]
-            partial = sums[b, v]
-            result = partial + weight * carry
-            scan_out[b, v] = result
-            parts = [ref[strip(b, v), :] for ref in values]
-            mean = mean_of(parts)
-            if b == 0 and v == 0:
-                head = result + ratio * mean
-            u = result - mean
-            suu += u * u
-            part_ua += u * weight
-            for m, part in enumerate(parts):
-                q = part - partial - weight * own_carries[m]
+            weight, partial = reach[b, v], sums[b, v]
+            error = None
+            for m, ref in enumerate(values):
+                q = ref[strip(b, v), :] - partial - weight * own_carries[m]
                 sqq[m] += q * q
                 part_qa[m] += q * weight
-        sua += part_ua * after
+                error = q if error is None else error + q
+            total += error * error
         for m in range(members):
             sqa[m] += part_qa[m] * after
+    suu = total / (members * members)
+    sua = -sum(sqa[1:], sqa[0]) / members
 
     def by_member(entries, m):
         found = entries[0]
@@ -315,7 +310,7 @@
 
 
 def returns_kernel(
-    moves_all, scan, reach, afters, stats, *refs
+    moves_all, sums, reach, carries, afters, stats, *refs
 ):
     members = lax.axis_size("member")
     values, refs = refs[:members], refs[members:]
@@ -342,9 +337,9 @@
     eps = spread(jnp.sum(own_eps, axis=1, keepdims=True), rows)
     eps = per_row(eps, rows)
     for b in range(count):
-        error = afters[b] * eps
+        carry = carries[b] + afters[b] * eps
         for v in range(CHUNK):
-            work[strip(b, v), :] = scan[b, v] + reach[b, v] * error
+            work[strip(b, v), :] = sums[b, v] + reach[b, v] * carry
         flat = jnp.concatenate(chunk_rows(work, b), axis=0).T
         for t in range(group):
             j = b * group + t
@@ -451,13 +446,12 @@
         )
     )
     rewards_turned, own_turned, decay, reach, powers, consts = kept
-    scan, afters, stats = pl.pallas_call(
+    sums, carries, afters, stats = pl.pallas_call(
         local_kernel,
-        out_shape=(strips, array(count, SUBLANES, LANES), array(rows, LANES)),
+        out_shape=(strips, *[array(count, SUBLANES, LANES)] * 2, array(rows, LANES)),
         in_specs=[VMEM] * (members + 5),
-        out_specs=(VMEM,) * 3,
+        out_specs=(VMEM,) * 4,
         scratch_shapes=[
-            pltpu.VMEM((count, CHUNK, SUBLANES, LANES), jnp.float32),
             pltpu.VMEM((SUBLANES * (SUBLANES + 1), LANES), jnp.float32),
         ]
         + [pltpu.VMEM((count * DEPTH, LANES), jnp.float32)] * (members - 1),
@@ -479,7 +473,7 @@
     returns, loss, raw, squares = pl.pallas_call(
         functools.partial(returns_kernel, float(moves_all)),
         out_shape=(block, array(1, rows), block, array(rows, LANES)),
-        in_specs=[VMEM] * (4 + members),
+        in_specs=[VMEM] * (5 + members),
         out_specs=(HBM, HBM, VMEM, VMEM),
         scratch_shapes=[
             pltpu.VMEM((rows, moves), jnp.float32),
@@ -490,7 +484,7 @@
         compiler_params=params,
         cost_estimate=pl.CostEstimate(flops=2000000, bytes_accessed=1000000, transcendentals=0),
         name="write_returns",
-    )(scan, reach, afters, stats, kept_own, *others)
+    )(sums, reach, carries, afters, stats, kept_own, *others)
     advantages = pl.pallas_call(
         functools.partial(scale_kernel, float(moves_all * rows * groups)),
         out_shape=block,

time: 18.3 us -> 18.2 us (level)
  no operation moved by 1% of the time
where the time goes in v5:
time: 18.2 us; the launch traced here: 18.1 us
  starting transfers between devices  9.37 us (51%)
  waiting for transfers between devices  4.35 us (24%)
  Pallas kernels  3.69 us (20%)
  between operations  0.66 us (4%)
    ppermute x4, starting transfers between devices, exchange(): return lax.ppermute(value, names, pairs)  8.81 us
    ppermute x4, waiting for transfers between devices, exchange(): return lax.ppermute(value, names, pairs)  4.35 us
    pallas_call x1, Pallas kernels, per_device(): pl.pallas_call(decay_kernel, out_shape=(block, flat, flat, strips, strips...  1.3 us
    pallas_call x1, Pallas kernels, per_device(): pl.pallas_call(functools.partial(returns_kernel, float(moves_all)), out_s...  0.96 us
    pallas_call x1, Pallas kernels, per_device(): pl.pallas_call(functools.partial(scale_kernel, float(moves_all * rows * g...  0.86 us
    pallas_call x1, Pallas kernels, per_device(): pl.pallas_call(local_kernel, out_shape=(strips, *[array(count, SUBLANES,...  0.58 us
    ppermute x1, starting transfers between devices, per_device(): lax.ppermute(own, 'member', [(m, (m + turn) % members) for m in range(mem...  0.56 us
  transfers between devices with their start and end apart: 5, of which 4 were waited for; matrix products, arithmetic and copies ran while one was open for 0% of the time, Pallas kernels for 12%

profile of v5, /device:TPU:0, one launch (start us, length us, event | category | flops | bytes accessed | tf_op | source)
XLA Modules:
  0.0 18.1 jit_solution(9555221276857760062)
XLA Ops:
  0.6 0.6 %collective-permute-start = (f32[8,4096]{1,0:T(8,128)}, f32[8,4096]{1,0:T(8,128)S(1)}, u32[]{:S(2)}, u32[]{:S(2)}) collective-permute-start(f32[8,4096]{1,0:T(8,128)} %bitcast.5), channel_id=1, source_target_pairs={{0,1},{1,0},{2,3},{3,2},{4,5},{5,4},{6,7},{7,6},{8,9},{9,8},{10,11... | collective-permute-start | bytes 393224 | tf_op jit(solution)/shard_map/ppermute | solution.py:408
  1.2 1.3 %decay_scan.1 = (f32[8,4096]{1,0:T(8,128)S(1)}, f32[272,128]{1,0:T(8,128)S(1)}, f32[272,128]{1,0:T(8,128)S(1)}, f32[2,16,8,128]{3,2,1,0:T(8,128)S(1)}, f32[2,16,...) custom-call(f32[8,4096]{1,0:T(8,128)} %rewards.1, s32[8,4096]{1,0:T(8,128)} %dones.1, ...), custom_call_target="tpu_custom_call" | custom-call | flops 4000000 | bytes 2000000 | tf_op jit(solution)/shard_map/decay_scan/pallas_call | solution.py:422
  2.5 0.0 collective-permute-done.refs_0_.refs_1_
  2.5 0.6 %local_scan.1 = (f32[2,16,8,128]{3,2,1,0:T(8,128)S(1)}, f32[2,8,128]{2,1,0:T(8,128)S(1)}, f32[2,8,128]{2,1,0:T(8,128)S(1)}, f32[8,128]{1,0:T(8,128)S(1)}) custom-call(f32[272,128]{1,0:T(8,128)S(1)} %get-tuple-element.18.rewards, f32[272,128]{1,0:T(8,128)S(1)} %get-tuple-element.19.own, f32[8,4096]{1,0:T(8,128)S(1)} %collective-permute-done.refs_0_.refs_1_, ...), custom_call_target="tpu_custom_call" | custom-call | tf_op jit(solution)/shard_map/local_scan/pallas_call | solution.py:449
  3.1 2.6 %collective-permute-start.1 = (f32[8,128]{1,0:T(8,128)S(1)}, f32[8,128]{1,0:T(8,128)S(1)}, u32[]{:S(2)}, u32[]{:S(2)}) collective-permute-start(f32[8,128]{1,0:T(8,128)S(1)} %get-tuple-element.27), channel_id=1, source_target_pairs={{0,9},{1,8},{2,11},{3,10},{4,13},{5,12},{6,15},{7,14},{8,1},{9,0},... | collective-permute-start | bytes 12296 | tf_op jit(solution)/shard_map/ppermute | solution.py:394
  5.7 1.3 %collective-permute-done.1 = f32[8,128]{1,0:T(8,128)S(1)} collective-permute-done((f32[8,128]{1,0:T(8,128)S(1)}, f32[8,128]{1,0:T(8,128)S(1)}, u32[]{:S(2)}, u32[]{:S(2)}) %collective-permute-start.1) | collective-permute-done | bytes 4128 | tf_op jit(solution)/shard_map/ppermute | solution.py:394
  7.0 1.7 %collective-permute-start.2 = (f32[8,128]{1,0:T(8,128)S(1)}, f32[8,128]{1,0:T(8,128)S(1)}, u32[]{:S(2)}, u32[]{:S(2)}) collective-permute-start(f32[8,128]{1,0:T(8,128)S(1)} %add.9), channel_id=1, source_target_pairs={{0,17},{1,16},{2,19},{3,18},{4,21},{5,20},{6,23},{7,22},{8,25},{9,... | collective-permute-start | bytes 12296 | tf_op jit(solution)/shard_map/ppermute | solution.py:394
  8.8 1.3 %collective-permute-done.2 = f32[8,128]{1,0:T(8,128)S(1)} collective-permute-done((f32[8,128]{1,0:T(8,128)S(1)}, f32[8,128]{1,0:T(8,128)S(1)}, u32[]{:S(2)}, u32[]{:S(2)}) %collective-permute-start.2) | collective-permute-done | bytes 4128 | tf_op jit(solution)/shard_map/ppermute | solution.py:394
  10.1 1.8 %collective-permute-start.3 = (f32[8,128]{1,0:T(8,128)S(1)}, f32[8,128]{1,0:T(8,128)S(1)}, u32[]{:S(2)}, u32[]{:S(2)}) collective-permute-start(f32[8,128]{1,0:T(8,128)S(1)} %add.10), channel_id=1, source_target_pairs={{0,3},{1,2},{2,1},{3,0},{4,7},{5,6},{6,5},{7,4},{8,11},{9,10},{10,... | collective-permute-start | bytes 12296 | tf_op jit(solution)/shard_map/ppermute | solution.py:394
  11.8 1.3 %collective-permute-done.3 = f32[8,128]{1,0:T(8,128)S(1)} collective-permute-done((f32[8,128]{1,0:T(8,128)S(1)}, f32[8,128]{1,0:T(8,128)S(1)}, u32[]{:S(2)}, u32[]{:S(2)}) %collective-permute-start.3) | collective-permute-done | bytes 4128 | tf_op jit(solution)/shard_map/ppermute | solution.py:394
  13.2 2.7 %collective-permute-start.4 = (f32[1,8,128]{2,1,0:T(8,128)S(1)}, f32[1,8,128]{2,1,0:T(8,128)S(1)}, u32[]{:S(2)}, u32[]{:S(2)}) collective-permute-start(f32[1,8,128]{2,1,0:T(8,128)S(1)} %bitcast.4), channel_id=1, source_target_pairs={{0,5},{1,4},{2,7},{3,6},{4,1},{5,0},{6,3},{7,2},{8,13},{9,12},{10,... | collective-permute-start | bytes 12296 | tf_op jit(solution)/shard_map/ppermute | solution.py:394
  15.9 1.0 %write_returns.1 = (f32[8,4096]{1,0:T(8,128)}, f32[1,8]{1,0:T(1,128)}, f32[8,4096]{1,0:T(8,128)S(1)}, f32[8,128]{1,0:T(8,128)S(1)}) custom-call(f32[2,16,8,128]{3,2,1,0:T(8,128)S(1)} %get-tuple-element.24.sums, f32[2,16,8,128]{3,2,1,0:T(8,128)S(1)} %get-tuple-element.21.refs_2_.reach, f32[2,8,128]{2,1,0:T(8,128)S(1)} %get-tuple-element.25.carries, ...), custom_call_target="tpu_custom_call" | custom-call | flops 2000000 | bytes 1000000 | tf_op jit(solution)/shard_map/write_returns/pallas_call | solution.py:473
  16.9 0.4 %collective-permute-done.4.refs_0_ = f32[1,8,128]{2,1,0:T(8,128)S(1)} collective-permute-done((f32[1,8,128]{2,1,0:T(8,128)S(1)}, f32[1,8,128]{2,1,0:T(8,128)S(1)}, u32[]{:S(2)}, u32[]{:S(2)}) %collective-permute-start.4) | collective-permute-done | bytes 4128 | tf_op jit(solution)/shard_map/ppermute | solution.py:394
  17.2 0.9 %scale.1 = f32[8,4096]{1,0:T(8,128)} custom-call(f32[8,4096]{1,0:T(8,128)S(1)} %get-tuple-element.30.raw, f32[8,128]{1,0:T(8,128)S(1)} %get-tuple-element.31.squares, f32[1,8,128]{2,1,0:T(8,128)S(1)} %collective-permute-done.4.refs_0_), custom_call_target="tpu_custom_call" | custom-call | tf_op jit(solution)/shard_map/scale/pallas_call | solution.py:488
  (3 shorter events, 0.0 us)
Async XLA Ops:
  0.6 1.9 %collective-permute-start = (f32[8,4096]{1,0:T(8,128)}, f32[8,4096]{1,0:T(8,128)S(1)}, u32[]{:S(2)}, u32[]{:S(2)}) collective-permute-start(f32[8,4096]{1,0:T(8,128)} %bitcast.5), channel_id=1, source_target_pairs={{0,1},{1,0},{2,3},{3,2},{4,5},{5,4},{6,7},{7,6},{8,9},{9,8},{10,11... | collective-permute-start | bytes 393224 | tf_op jit(solution)/shard_map/ppermute | solution.py:408
  3.1 3.9 %collective-permute-start.1 = (f32[8,128]{1,0:T(8,128)S(1)}, f32[8,128]{1,0:T(8,128)S(1)}, u32[]{:S(2)}, u32[]{:S(2)}) collective-permute-start(f32[8,128]{1,0:T(8,128)S(1)} %get-tuple-element.27), channel_id=1, source_target_pairs={{0,9},{1,8},{2,11},{3,10},{4,13},{5,12},{6,15},{7,14},{8,1},{9,0},... | collective-permute-start | bytes 12296 | tf_op jit(solution)/shard_map/ppermute | solution.py:394
  7.0 3.1 %collective-permute-start.2 = (f32[8,128]{1,0:T(8,128)S(1)}, f32[8,128]{1,0:T(8,128)S(1)}, u32[]{:S(2)}, u32[]{:S(2)}) collective-permute-start(f32[8,128]{1,0:T(8,128)S(1)} %add.9), channel_id=1, source_target_pairs={{0,17},{1,16},{2,19},{3,18},{4,21},{5,20},{6,23},{7,22},{8,25},{9,... | collective-permute-start | bytes 12296 | tf_op jit(solution)/shard_map/ppermute | solution.py:394
  10.1 3.1 %collective-permute-start.3 = (f32[8,128]{1,0:T(8,128)S(1)}, f32[8,128]{1,0:T(8,128)S(1)}, u32[]{:S(2)}, u32[]{:S(2)}) collective-permute-start(f32[8,128]{1,0:T(8,128)S(1)} %add.10), channel_id=1, source_target_pairs={{0,3},{1,2},{2,1},{3,0},{4,7},{5,6},{6,5},{7,4},{8,11},{9,10},{10,... | collective-permute-start | bytes 12296 | tf_op jit(solution)/shard_map/ppermute | solution.py:394
  13.2 4.0 %collective-permute-start.4 = (f32[1,8,128]{2,1,0:T(8,128)S(1)}, f32[1,8,128]{2,1,0:T(8,128)S(1)}, u32[]{:S(2)}, u32[]{:S(2)}) collective-permute-start(f32[1,8,128]{2,1,0:T(8,128)S(1)} %bitcast.4), channel_id=1, source_target_pairs={{0,5},{1,4},{2,7},{3,6},{4,1},{5,0},{6,3},{7,2},{8,13},{9,12},{10,... | collective-permute-start | bytes 12296 | tf_op jit(solution)/shard_map/ppermute | solution.py:394
